TPU v7x, 768 devices: a whole 4x8x12 slice. The times are simulated.
768 devices in a mesh: ctx: 12 (over z), ch: 64 (over x, y, core).
Axes of the slice: x: 4, y: 8, z: 12, core: 2. Of those that a mesh axis runs over, the one named last changes fastest.
Arguments:
- stream: bfloat16 [1536, 8192], P('ctx', 'ch'), may hold values from -6 to 6
- in_weight: bfloat16 [8192, 3, 8192], P(None, None, 'ch'), may hold values from -0.0625 to 0.0625
- pole_rate: float32 [8192, 16], P('ch'), may hold values from 0.00032552084 to 0.05
- residue: float32 [8192, 16], P('ch'), may hold values from -1.5 to 1.5
- skip_gain: float32 [8192], P('ch'), may hold values from -4 to 4
- doc_lengths: int32 [8], replicated, may hold values from 1 to 768, 1536 in all
Outputs:
- mixed: bfloat16 [1536, 8192], P('ctx', 'ch')
Inputs may be any that keep to these rules, and one draw needn't show every extreme that they name: `doc_lengths`: the 8 documents lie end to end and cover the row: the lengths sum to 1536, and the longest has exactly 1536 // 2 tokens.
All inputs are finite; a program needn't handle non-finite values.
Results may differ from a plain program's by a relative error of at most 0.003.
Values may be sent and summed in bfloat16 or wider, within the bound.
A program may use at most 64 MiB of HBM per device.

v0:
```python
import jax
import jax.numpy as jnp
from jax import lax
from jax.sharding import PartitionSpec as P


def shifted(block, axis, distance):
    devices = range(lax.axis_size(axis))
    route = [(i - distance, i) for i in devices if i - distance in devices]
    return lax.ppermute(block, axis, route)


def combine(earlier, later):
    return (earlier[0] * later[0], later[0] * earlier[1] + later[1])


def split_proj(product, squares, width, local):
    rowscale = lax.rsqrt(squares / width + 1e-06)
    proj = product * rowscale[:, None]
    outer = proj[:, :local]
    driven = proj[:, local : 2 * local] * proj[:, 2 * local :]
    return (outer, driven)


def local_scan(driven, keep, lam):
    modes, local = lam.shape
    decay = keep[:, None, None] * lam[None, :, :]
    drive = jnp.broadcast_to(driven[:, None, :], (driven.shape[0], modes, local))
    return lax.associative_scan(combine, (decay, drive), axis=0)


def per_device(stream, in_weight, pole_rate, residue, skip_gain, doc_lengths):
    rows = stream.shape[0]
    width = in_weight.shape[0]
    local = in_weight.shape[2]
    modes = pole_rate.shape[1]
    weights = in_weight.reshape(width, 3 * local)
    lam = jnp.exp(-pole_rate).T
    mix = (residue * jnp.sqrt(-jnp.expm1(-2.0 * pole_rate))).T
    starts = jnp.cumsum(doc_lengths) - doc_lengths
    position = lax.axis_index("ctx") * rows + jnp.arange(rows, dtype=jnp.int32)
    is_start = jnp.any(position[:, None] == starts[None, :], axis=1)
    keep = jnp.where(is_start, 0.0, 1.0).astype(jnp.float32)
    whole = lax.all_gather(stream, "ch", axis=1, tiled=True)
    floats = whole.astype(jnp.float32)
    squares = jnp.sum(floats * floats, axis=1)
    product = jnp.dot(whole, weights, preferred_element_type=jnp.float32)
    outer, driven = split_proj(product, squares, width, local)
    decay_cum, local_state = local_scan(driven, keep, lam)
    block_decay = decay_cum[-1]
    block_state = local_state[-1]
    zeros_state = jnp.zeros((modes, local), jnp.float32)

    def forward(step, incoming):
        outgoing = block_decay * incoming + block_state
        return shifted(outgoing, "ctx", 1)

    incoming = lax.fori_loop(0, lax.axis_size("ctx") - 1, forward, zeros_state)
    state = local_state + decay_cum * incoming[None, :, :]
    filtered = jnp.einsum("tnc,nc->tc", state, mix)
    return (outer * (filtered + skip_gain[None, :] * driven)).astype(jnp.bfloat16)


def solution(mesh):
    placed = (P("ctx", "ch"), P(None, None, "ch"), P("ch", None), P("ch", None), P("ch"), P())
    return jax.shard_map(
        per_device, mesh=mesh, in_specs=placed, out_specs=P("ctx", "ch"), check_vma=False
    )
```

profile of v0, /device:TPU:192, one launch (start us, length us, event | category | flops | bytes accessed | tf_op | source)
XLA Modules:
  0.0 304.7 jit_solution(14645019880994475622)
XLA Ops:
  6.5 0.7 all-gather.2.cloned.1.call-update
  7.3 8.8 %copy.8 = bf16[8192,3,128]{0,2,1:T(8,128)(2,1)} copy(bf16[8192,3,128]{2,0,1:T(8,128)(2,1)} %param.9) | data formatting | bytes 12582912 | tf_op args[1]
  16.0 0.2 reduce-window.9
  16.2 0.1 compare_reduce_fusion
  16.3 0.6 sqrt_multiply_fusion
  17.0 0.2 broadcast_multiply_fusion
  17.2 81.7 %all-gather.2.cloned.1.call-done = bf16[128,8192]{1,0:T(8,128)(2,1)} async-done(((bf16[128,128]{1,0:T(8,128)(2,1)}), bf16[128,8192]{1,0:T(8,128)(2,1)}) %all-gather.2.cloned.1.call-update) | async-done | bytes 2097168 | tf_op jit(solution)/shard_map/all_gather | solution.py:44
  98.9 2.1 multiply_reduce_fusion
  101.0 5.4 %convolution_multiply_fusion = f32[128,384]{1,0:T(8,128)S(1)} fusion(bf16[128,8192]{1,0:T(8,128)(2,1)} %all-gather.2.cloned.1.call-done, bf16[8192,384]{0,1:T(8,128)(2,1)} %bitcast.23, f32[128]{0:T(128)S(1)} %add_rsqrt_fusion), kind=kOutput, calls=%fused_computation.2 | convolution fusion | flops 805355520 | bytes 8585728 | tf_op jit(solution)/shard_map/dot_general | solution.py:47
  106.4 0.1 multiply_add_fusion.1
  106.5 0.1 slice_add_fusion
  107.2 0.7 fusion.4
  107.9 0.6 slice.320
  108.6 0.8 pad_maximum_fusion.6
  109.6 0.7 fusion.2
  110.3 0.7 add.186
  111.0 0.7 pad_maximum_fusion.5
  111.7 0.1 pad.108
  111.8 0.1 pad.109
  112.0 5.6 %pad.95 = f32[32,16,128]{2,1,0:T(8,128)S(1)} pad(f32[16,16,128]{2,1,0:T(8,128)} %add.186, f32[]{:T(128)} %constant.4.clone.1), padding=1_0_1x0_0_0x0_0_0 | pad | bytes 393220 | tf_op jit(solution)/shard_map/pad | solution.py:29
  117.6 0.9 pad_maximum_fusion.4
  118.5 0.1 pad.94
  118.6 0.7 add.188
  119.4 0.9 fusion.1
  120.3 0.7 add.197
  121.0 1.0 pad_maximum_fusion.2
  122.0 0.3 pad.96
  122.3 11.2 %pad.97 = f32[64,16,128]{2,1,0:T(8,128)S(1)} pad(f32[32,16,128]{2,1,0:T(8,128)} %add.188, f32[]{:T(128)} %constant.4.clone.1), padding=1_0_1x0_0_0x0_0_0 | pad | bytes 786436 | tf_op jit(solution)/shard_map/pad | solution.py:29
  133.5 0.1 add.190
  133.5 20.0 %pad.99 = f32[128,16,128]{2,1,0:T(8,128)} pad(f32[64,16,128]{2,1,0:T(8,128)S(1)} %add.190, f32[]{:T(128)} %constant.4.clone.1), padding=1_0_1x0_0_0x0_0_0 | pad | bytes 1572868 | tf_op jit(solution)/shard_map/pad | solution.py:29
  153.6 0.3 pad.110
  153.9 11.2 %pad.111 = f32[64,16,128]{2,1,0:T(8,128)S(1)} pad(f32[32,16,128]{2,1,0:T(8,128)} %add.197, f32[]{:T(128)} %constant.4.clone.1), padding=1_0_1x0_0_0x0_0_0 | pad | bytes 786436 | tf_op jit(solution)/shard_map/pad | solution.py:29
  165.1 0.9 add.198
  165.9 1.0 fusion
  167.0 0.5 pad.98
  167.5 22.4 %pad.113 = f32[128,16,128]{2,1,0:T(8,128)S(1)} pad(f32[64,16,128]{2,1,0:T(8,128)} %add.198, f32[]{:T(128)} %constant.4.clone.1), padding=1_0_1x0_0_0x0_0_0 | pad | bytes 1572868 | tf_op jit(solution)/shard_map/pad | solution.py:29
  189.9 1.9 pad_maximum_fusion.1
  191.8 29.4 %pad.112 = f32[128,16,128]{2,1,0:T(8,128)} pad(f32[64,16,128]{2,1,0:T(8,128)} %pad_maximum_fusion.1, f32[]{:T(128)} %constant.4.clone.1), padding=0_1_1x0_0_0x0_0_0 | pad | bytes 1572868 | tf_op jit(solution)/shard_map/pad | solution.py:29
  221.1 0.7 add_bitcast_fusion.1
  221.8 73.6 %while.10 = (s32[]{:T(128)}, f32[16,128]{1,0:T(8,128)S(1)}, f32[16,128]{1,0:T(8,128)S(1)}, f32[16,128]{1,0:T(8,128)S(1)}, s32[]{:T(128)}) while((s32[]{:T(128)}, f32[16,128]{1,0:T(8,128)S(1)}, f32[16,128]{1,0:T(8,128)S(1)}, f32[16,128]{1,0:T(8,128)S(1)}, s32[]{:T(128)}) %tuple.38), condition=%wide.region_4.5_spmd, body=%wide.region_3.4_spmd.sunk | while | flops 4098 | bytes 65637 | solution.py:58
  221.8 4.8 %collective-permute-start = (f32[16,128]{1,0:T(8,128)S(1)}, f32[16,128]{1,0:T(8,128)S(1)}, u32[]{:S(2)}, u32[]{:S(2)}) collective-permute-start(f32[16,128]{1,0:T(8,128)S(1)} %multiply_add_fusion.3), channel_id=1, source_target_pairs={{0,64},{64,128},{128,192},{192,256},{256,320},{320,384},{384,448},... | collective-permute-start | bytes 24584 | tf_op jit(solution)/shard_map/while/body/eval_jaxpr/ppermute | solution.py:10
  226.6 1.3 collective-permute-done
  228.0 5.4 %collective-permute-start = (f32[16,128]{1,0:T(8,128)S(1)}, f32[16,128]{1,0:T(8,128)S(1)}, u32[]{:S(2)}, u32[]{:S(2)}) collective-permute-start(f32[16,128]{1,0:T(8,128)S(1)} %multiply_add_fusion.3), channel_id=1, source_target_pairs={{0,64},{64,128},{128,192},{192,256},{256,320},{320,384},{384,448},... | collective-permute-start | bytes 24584 | tf_op jit(solution)/shard_map/while/body/eval_jaxpr/ppermute | solution.py:10
  233.4 1.3 collective-permute-done
  234.7 5.4 %collective-permute-start = (f32[16,128]{1,0:T(8,128)S(1)}, f32[16,128]{1,0:T(8,128)S(1)}, u32[]{:S(2)}, u32[]{:S(2)}) collective-permute-start(f32[16,128]{1,0:T(8,128)S(1)} %multiply_add_fusion.3), channel_id=1, source_target_pairs={{0,64},{64,128},{128,192},{192,256},{256,320},{320,384},{384,448},... | collective-permute-start | bytes 24584 | tf_op jit(solution)/shard_map/while/body/eval_jaxpr/ppermute | solution.py:10
  240.1 1.3 collective-permute-done
  241.5 5.4 %collective-permute-start = (f32[16,128]{1,0:T(8,128)S(1)}, f32[16,128]{1,0:T(8,128)S(1)}, u32[]{:S(2)}, u32[]{:S(2)}) collective-permute-start(f32[16,128]{1,0:T(8,128)S(1)} %multiply_add_fusion.3), channel_id=1, source_target_pairs={{0,64},{64,128},{128,192},{192,256},{256,320},{320,384},{384,448},... | collective-permute-start | bytes 24584 | tf_op jit(solution)/shard_map/while/body/eval_jaxpr/ppermute | solution.py:10
  246.9 1.3 collective-permute-done
  248.2 5.4 %collective-permute-start = (f32[16,128]{1,0:T(8,128)S(1)}, f32[16,128]{1,0:T(8,128)S(1)}, u32[]{:S(2)}, u32[]{:S(2)}) collective-permute-start(f32[16,128]{1,0:T(8,128)S(1)} %multiply_add_fusion.3), channel_id=1, source_target_pairs={{0,64},{64,128},{128,192},{192,256},{256,320},{320,384},{384,448},... | collective-permute-start | bytes 24584 | tf_op jit(solution)/shard_map/while/body/eval_jaxpr/ppermute | solution.py:10
  253.6 1.3 collective-permute-done
  255.0 5.4 %collective-permute-start = (f32[16,128]{1,0:T(8,128)S(1)}, f32[16,128]{1,0:T(8,128)S(1)}, u32[]{:S(2)}, u32[]{:S(2)}) collective-permute-start(f32[16,128]{1,0:T(8,128)S(1)} %multiply_add_fusion.3), channel_id=1, source_target_pairs={{0,64},{64,128},{128,192},{192,256},{256,320},{320,384},{384,448},... | collective-permute-start | bytes 24584 | tf_op jit(solution)/shard_map/while/body/eval_jaxpr/ppermute | solution.py:10
  260.4 1.3 collective-permute-done
  261.7 5.4 %collective-permute-start = (f32[16,128]{1,0:T(8,128)S(1)}, f32[16,128]{1,0:T(8,128)S(1)}, u32[]{:S(2)}, u32[]{:S(2)}) collective-permute-start(f32[16,128]{1,0:T(8,128)S(1)} %multiply_add_fusion.3), channel_id=1, source_target_pairs={{0,64},{64,128},{128,192},{192,256},{256,320},{320,384},{384,448},... | collective-permute-start | bytes 24584 | tf_op jit(solution)/shard_map/while/body/eval_jaxpr/ppermute | solution.py:10
  267.1 1.3 collective-permute-done
  268.5 5.4 %collective-permute-start = (f32[16,128]{1,0:T(8,128)S(1)}, f32[16,128]{1,0:T(8,128)S(1)}, u32[]{:S(2)}, u32[]{:S(2)}) collective-permute-start(f32[16,128]{1,0:T(8,128)S(1)} %multiply_add_fusion.3), channel_id=1, source_target_pairs={{0,64},{64,128},{128,192},{192,256},{256,320},{320,384},{384,448},... | collective-permute-start | bytes 24584 | tf_op jit(solution)/shard_map/while/body/eval_jaxpr/ppermute | solution.py:10
  273.9 1.3 collective-permute-done
  275.2 5.4 %collective-permute-start = (f32[16,128]{1,0:T(8,128)S(1)}, f32[16,128]{1,0:T(8,128)S(1)}, u32[]{:S(2)}, u32[]{:S(2)}) collective-permute-start(f32[16,128]{1,0:T(8,128)S(1)} %multiply_add_fusion.3), channel_id=1, source_target_pairs={{0,64},{64,128},{128,192},{192,256},{256,320},{320,384},{384,448},... | collective-permute-start | bytes 24584 | tf_op jit(solution)/shard_map/while/body/eval_jaxpr/ppermute | solution.py:10
  280.6 1.3 collective-permute-done
  282.0 5.4 %collective-permute-start = (f32[16,128]{1,0:T(8,128)S(1)}, f32[16,128]{1,0:T(8,128)S(1)}, u32[]{:S(2)}, u32[]{:S(2)}) collective-permute-start(f32[16,128]{1,0:T(8,128)S(1)} %multiply_add_fusion.3), channel_id=1, source_target_pairs={{0,64},{64,128},{128,192},{192,256},{256,320},{320,384},{384,448},... | collective-permute-start | bytes 24584 | tf_op jit(solution)/shard_map/while/body/eval_jaxpr/ppermute | solution.py:10
  287.4 1.3 collective-permute-done
  288.7 5.4 %collective-permute-start = (f32[16,128]{1,0:T(8,128)S(1)}, f32[16,128]{1,0:T(8,128)S(1)}, u32[]{:S(2)}, u32[]{:S(2)}) collective-permute-start(f32[16,128]{1,0:T(8,128)S(1)} %multiply_add_fusion.3), channel_id=1, source_target_pairs={{0,64},{64,128},{128,192},{192,256},{256,320},{320,384},{384,448},... | collective-permute-start | bytes 24584 | tf_op jit(solution)/shard_map/while/body/eval_jaxpr/ppermute | solution.py:10
  294.1 1.3 collective-permute-done
  295.5 1.8 multiply_reduce_fusion.1
  297.2 0.6 fusion.3
  (80 shorter events, 0.9 us)
Async XLA Ops:
  6.5 92.3 %all-gather.2.cloned.1.call-start = ((), (), s32[]{:S(2)}) async-start(), calls=%async_computation | async-start | bytes 2129920 | tf_op jit(solution)/shard_map/all_gather | solution.py:44
  7.3 8.8 %copy-start.7 = (s32[8]{0:T(128)S(1)}, s32[8]{0:T(128)}, u32[]{:S(2)}) copy-start(s32[8]{0:T(128)} %param.13) | copy-start | bytes 100
  7.3 9.1 %copy-start.4 = (f32[128,16]{0,1:T(8,128)S(1)}, f32[128,16]{0,1:T(8,128)}, u32[]{:S(2)}) copy-start(f32[128,16]{0,1:T(8,128)} %param.11) | copy-start | bytes 24580
  7.3 9.1 %copy-start.5 = (f32[128,16]{0,1:T(8,128)S(1)}, f32[128,16]{0,1:T(8,128)}, u32[]{:S(2)}) copy-start(f32[128,16]{0,1:T(8,128)} %param.10) | copy-start | bytes 24580
  17.2 148.8 %copy-start = (f32[128,16,128]{2,1,0:T(8,128)}, f32[128,16,128]{2,1,0:T(8,128)S(1)}, u32[]{:S(2)}) copy-start(f32[128,16,128]{2,1,0:T(8,128)S(1)} %broadcast_multiply_fusion) | copy-start | bytes 3145732
  120.3 33.3 %copy-start.2 = (f32[31,16,128]{2,1,0:T(8,128)S(1)}, f32[31,16,128]{2,1,0:T(8,128)}, u32[]{:S(2)}) copy-start(f32[31,16,128]{2,1,0:T(8,128)} %get-tuple-element.41) | copy-start | bytes 761860
  166.9 23.0 %slice-start = ((f32[128,16,128]{2,1,0:T(8,128)}), f32[1,16,128]{2,1,0:T(8,128)S(1)}, s32[]{:S(2)}) async-start(f32[128,16,128]{2,1,0:T(8,128)} %copy-done), calls=%async_computation.1 | async-start | bytes 16384 | tf_op jit(solution)/shard_map/slice | solution.py:29
  166.9 54.2 %copy-start.1 = (f32[128,16,128]{2,1,0:T(8,128)S(1)}, f32[128,16,128]{2,1,0:T(8,128)}, u32[]{:S(2)}) copy-start(f32[128,16,128]{2,1,0:T(8,128)} %pad.99) | copy-start | bytes 3145732
  166.9 128.5 %copy-start.3 = (f32[128,16]{0,1:T(8,128)S(1)}, f32[128,16]{0,1:T(8,128)}, u32[]{:S(2)}) copy-start(f32[128,16]{0,1:T(8,128)} %get-tuple-element.66) | copy-start | bytes 24580
  167.5 129.7 %copy-start.6 = (f32[128]{0:T(128)S(1)}, f32[128]{0:T(128)}, u32[]{:S(2)}) copy-start(f32[128]{0:T(128)} %param.12) | copy-start | bytes 1540
  221.8 6.1 %collective-permute-start = (f32[16,128]{1,0:T(8,128)S(1)}, f32[16,128]{1,0:T(8,128)S(1)}, u32[]{:S(2)}, u32[]{:S(2)}) collective-permute-start(f32[16,128]{1,0:T(8,128)S(1)} %multiply_add_fusion.3), channel_id=1, source_target_pairs={{0,64},{64,128},{128,192},{192,256},{256,320},{320,384},{384,448},... | collective-permute-start | bytes 24584 | tf_op jit(solution)/shard_map/while/body/eval_jaxpr/ppermute | solution.py:10
  228.0 6.7 %collective-permute-start = (f32[16,128]{1,0:T(8,128)S(1)}, f32[16,128]{1,0:T(8,128)S(1)}, u32[]{:S(2)}, u32[]{:S(2)}) collective-permute-start(f32[16,128]{1,0:T(8,128)S(1)} %multiply_add_fusion.3), channel_id=1, source_target_pairs={{0,64},{64,128},{128,192},{192,256},{256,320},{320,384},{384,448},... | collective-permute-start | bytes 24584 | tf_op jit(solution)/shard_map/while/body/eval_jaxpr/ppermute | solution.py:10
  234.7 6.7 %collective-permute-start = (f32[16,128]{1,0:T(8,128)S(1)}, f32[16,128]{1,0:T(8,128)S(1)}, u32[]{:S(2)}, u32[]{:S(2)}) collective-permute-start(f32[16,128]{1,0:T(8,128)S(1)} %multiply_add_fusion.3), channel_id=1, source_target_pairs={{0,64},{64,128},{128,192},{192,256},{256,320},{320,384},{384,448},... | collective-permute-start | bytes 24584 | tf_op jit(solution)/shard_map/while/body/eval_jaxpr/ppermute | solution.py:10
  241.5 6.7 %collective-permute-start = (f32[16,128]{1,0:T(8,128)S(1)}, f32[16,128]{1,0:T(8,128)S(1)}, u32[]{:S(2)}, u32[]{:S(2)}) collective-permute-start(f32[16,128]{1,0:T(8,128)S(1)} %multiply_add_fusion.3), channel_id=1, source_target_pairs={{0,64},{64,128},{128,192},{192,256},{256,320},{320,384},{384,448},... | collective-permute-start | bytes 24584 | tf_op jit(solution)/shard_map/while/body/eval_jaxpr/ppermute | solution.py:10
  248.2 6.7 %collective-permute-start = (f32[16,128]{1,0:T(8,128)S(1)}, f32[16,128]{1,0:T(8,128)S(1)}, u32[]{:S(2)}, u32[]{:S(2)}) collective-permute-start(f32[16,128]{1,0:T(8,128)S(1)} %multiply_add_fusion.3), channel_id=1, source_target_pairs={{0,64},{64,128},{128,192},{192,256},{256,320},{320,384},{384,448},... | collective-permute-start | bytes 24584 | tf_op jit(solution)/shard_map/while/body/eval_jaxpr/ppermute | solution.py:10
  255.0 6.7 %collective-permute-start = (f32[16,128]{1,0:T(8,128)S(1)}, f32[16,128]{1,0:T(8,128)S(1)}, u32[]{:S(2)}, u32[]{:S(2)}) collective-permute-start(f32[16,128]{1,0:T(8,128)S(1)} %multiply_add_fusion.3), channel_id=1, source_target_pairs={{0,64},{64,128},{128,192},{192,256},{256,320},{320,384},{384,448},... | collective-permute-start | bytes 24584 | tf_op jit(solution)/shard_map/while/body/eval_jaxpr/ppermute | solution.py:10
  261.7 6.7 %collective-permute-start = (f32[16,128]{1,0:T(8,128)S(1)}, f32[16,128]{1,0:T(8,128)S(1)}, u32[]{:S(2)}, u32[]{:S(2)}) collective-permute-start(f32[16,128]{1,0:T(8,128)S(1)} %multiply_add_fusion.3), channel_id=1, source_target_pairs={{0,64},{64,128},{128,192},{192,256},{256,320},{320,384},{384,448},... | collective-permute-start | bytes 24584 | tf_op jit(solution)/shard_map/while/body/eval_jaxpr/ppermute | solution.py:10
  268.5 6.7 %collective-permute-start = (f32[16,128]{1,0:T(8,128)S(1)}, f32[16,128]{1,0:T(8,128)S(1)}, u32[]{:S(2)}, u32[]{:S(2)}) collective-permute-start(f32[16,128]{1,0:T(8,128)S(1)} %multiply_add_fusion.3), channel_id=1, source_target_pairs={{0,64},{64,128},{128,192},{192,256},{256,320},{320,384},{384,448},... | collective-permute-start | bytes 24584 | tf_op jit(solution)/shard_map/while/body/eval_jaxpr/ppermute | solution.py:10
  275.2 6.7 %collective-permute-start = (f32[16,128]{1,0:T(8,128)S(1)}, f32[16,128]{1,0:T(8,128)S(1)}, u32[]{:S(2)}, u32[]{:S(2)}) collective-permute-start(f32[16,128]{1,0:T(8,128)S(1)} %multiply_add_fusion.3), channel_id=1, source_target_pairs={{0,64},{64,128},{128,192},{192,256},{256,320},{320,384},{384,448},... | collective-permute-start | bytes 24584 | tf_op jit(solution)/shard_map/while/body/eval_jaxpr/ppermute | solution.py:10
  282.0 6.7 %collective-permute-start = (f32[16,128]{1,0:T(8,128)S(1)}, f32[16,128]{1,0:T(8,128)S(1)}, u32[]{:S(2)}, u32[]{:S(2)}) collective-permute-start(f32[16,128]{1,0:T(8,128)S(1)} %multiply_add_fusion.3), channel_id=1, source_target_pairs={{0,64},{64,128},{128,192},{192,256},{256,320},{320,384},{384,448},... | collective-permute-start | bytes 24584 | tf_op jit(solution)/shard_map/while/body/eval_jaxpr/ppermute | solution.py:10
  288.7 6.7 %collective-permute-start = (f32[16,128]{1,0:T(8,128)S(1)}, f32[16,128]{1,0:T(8,128)S(1)}, u32[]{:S(2)}, u32[]{:S(2)}) collective-permute-start(f32[16,128]{1,0:T(8,128)S(1)} %multiply_add_fusion.3), channel_id=1, source_target_pairs={{0,64},{64,128},{128,192},{192,256},{256,320},{320,384},{384,448},... | collective-permute-start | bytes 24584 | tf_op jit(solution)/shard_map/while/body/eval_jaxpr/ppermute | solution.py:10
Sparse Core Ops, SparseCore 0:
  11.1 87.7 all-gather.1
where the time goes:
time: 311 us; the launch traced here: 305 us
  local copies, waits for them, and re-layouts  111 us (36%)
  waiting for transfers between devices  97.1 us (31%)
  starting transfers between devices  58.7 us (19%)
  other arithmetic  18.4 us (6%)
  between operations  13.8 us (4%)
  matrix products  5.41 us (2%)
    pad x24, local copies, waits for them, and re-layouts, local_scan(): return lax.associative_scan(combine, (decay, drive), axis=0)  102 us
    all_gather x1, waiting for transfers between devices, per_device(): whole = lax.all_gather(stream, 'ch', axis=1, tiled=True)  81.7 us
    ppermute x11, starting transfers between devices, shifted(): return lax.ppermute(block, axis, route)  58.7 us
    ppermute x11, waiting for transfers between devices, shifted(): return lax.ppermute(block, axis, route)  14.8 us
    unnamed x17, local copies, waits for them, and re-layouts  8.78 us
  transfers between devices with their start and end apart: 12, of which 12 were waited for; matrix products, arithmetic and copies ran while one was open for 3% of the time, Pallas kernels for 0%

commit v1 on v0

v1 whole, which is shorter than its diff:
```python
import functools

import jax
import jax.numpy as jnp
from jax import lax
from jax.experimental import pallas as pl
from jax.experimental.pallas import tpu as pltpu
from jax.sharding import PartitionSpec as P

MESH = pl.DeviceIdType.MESH
NX, NY = 4, 8
ROWS = 128
LOCAL = 128
MODES = 16
ROWS_A = 64
ROWS_B = ROWS - ROWS_A
REACH = 6
F32 = jnp.float32


def kernel(
    n_ctx, width,
    stream, w3, pole_h, resid_h, skip_h, docs_h, out,
    ga, gb, w, acc, sq, drv, y8, sw, lk, t2, pole, resid, skip, mine, got, gains, docs,
    w_sem, prm_sem, own_sem,
    a1_send, a1_recv, b1_send, b1_recv,
    ar_send, ar_recv, al_send, al_recv,
    br_send, br_recv, bl_send, bl_recv,
    as_send, as_recv, bs_send, bs_recv,
    z_send, z_recv,
):
    block = lax.axis_index("ctx")
    ch = lax.axis_index("ch")
    core = lax.rem(ch, 2)
    y = lax.rem(ch // 2, NY)
    x = ch // (2 * NY)

    def at(px, py, pc):
        return {"ch": (px * NY + py) * 2 + pc}

    def along_x(k):
        return lax.rem(x + (k + NX), NX)

    def along_y(k):
        return lax.rem(y + (k + NY), NY)

    def along_z(k):
        return lax.rem(block + (k + n_ctx), n_ctx)

    def remote(src, dst, send, recv, device):
        return pltpu.make_async_remote_copy(
            src_ref=src, dst_ref=dst, send_sem=send, recv_sem=recv,
            device_id=device, device_id_type=MESH,
        )

    parts = [
        pltpu.make_async_copy(w3.at[j], w.at[:, pl.ds(j * LOCAL, LOCAL)], w_sem.at[j])
        for j in range(3)
    ]
    params = [
        pltpu.make_async_copy(src, dst, prm_sem.at[i])
        for i, (src, dst) in enumerate(
            ((pole_h, pole), (resid_h, resid), (skip_h, skip), (docs_h, docs))
        )
    ]
    own_a = pltpu.make_async_copy(stream.at[pl.ds(0, ROWS_A)], ga.at[y, core, x], own_sem.at[0])
    own_b = pltpu.make_async_copy(stream.at[pl.ds(ROWS_A, ROWS_B)], gb.at[x, core, y], own_sem.at[1])
    own_a.start()
    own_b.start()
    for p in params:
        p.start()

    sibling = at(x, y, 1 - core)
    z_offsets = sorted({k % n_ctx for d in range(1, REACH + 1) for k in (d, -d)})
    friends = [sibling]
    friends += [at(along_x(k), y, core) for k in range(1, NX)]
    friends += [at(x, along_y(k), core) for k in range(1, NY)]
    friends += [{"ctx": along_z(k)} for k in z_offsets]
    barrier = pltpu.get_barrier_semaphore()
    for friend in friends:
        pl.semaphore_signal(barrier, inc=1, device_id=friend, device_id_type=MESH)
    for p in parts:
        p.start()
    pl.semaphore_wait(barrier, len(friends))

    a1 = [
        remote(stream.at[pl.ds(0, ROWS_A)], ga.at[y, core, x],
               a1_send.at[k - 1], a1_recv.at[k - 1], at(along_x(k), y, core))
        for k in range(1, NX)
    ]
    b1 = {
        k: remote(stream.at[pl.ds(ROWS_A, ROWS_B)], gb.at[x, core, y],
                  b1_send.at[k - 1], b1_recv.at[k - 1], at(x, along_y(k), core))
        for k in range(1, NY)
    }
    for c in a1:
        c.start()
    for k in (1, 7, 2, 6, 3, 5, 4):
        b1[k].start()

    sent = []

    def go(copy):
        copy.start()
        sent.append(copy)

    def a_right(step, lo, hi, group):
        ref = ga.at[group, core, pl.ds(lo, hi - lo)]
        return remote(ref, ref, ar_send.at[step], ar_recv.at[step], at(x, along_y(1), core))

    def a_left(step, lo, hi, group):
        ref = ga.at[group, core, pl.ds(lo, hi - lo)]
        return remote(ref, ref, al_send.at[step], al_recv.at[step], at(x, along_y(-1), core))

    def b_right(step, lo, hi, group):
        ref = gb.at[group, core, pl.ds(lo, hi - lo)]
        return remote(ref, ref, br_send.at[step], br_recv.at[step], at(along_x(1), y, core))

    def b_left(step, lo, hi, group):
        ref = gb.at[group, core, pl.ds(lo, hi - lo)]
        return remote(ref, ref, bl_send.at[step], bl_recv.at[step], at(along_x(-1), y, core))

    def a_sib(k, group, c):
        ref = ga.at[group, c]
        return remote(ref, ref, as_send.at[k], as_recv.at[k], sibling)

    def b_sib(k, group, c):
        ref = gb.at[group, c]
        return remote(ref, ref, bs_send.at[k], bs_recv.at[k], sibling)

    def add_group(buf, group, count, base, stride, lo, rows):
        def body(i, carry):
            total, squares = carry
            lhs = jnp.concatenate([buf[group, 0, i], buf[group, 1, i]], axis=1)
            first = pl.multiple_of(base + i * stride, 2 * LOCAL)
            total = total + jnp.dot(lhs, w[pl.ds(first, 2 * LOCAL), :], preferred_element_type=F32)
            f = lhs.astype(F32)
            f = f * f
            return total, squares + (f[:, :LOCAL] + f[:, LOCAL:])

        where = pl.ds(lo, rows)
        total, squares = lax.fori_loop(0, count, body, (acc[where, :], sq[where, :]))
        acc[where, :] = total
        sq[where, :] = squares

    def dots_a(k):
        group = along_y(k)
        add_group(ga, group, NX, group * (2 * LOCAL), NY * 2 * LOCAL, 0, ROWS_A)

    def dots_b(k):
        group = along_x(k)
        add_group(gb, group, NY, group * (NY * 2 * LOCAL), 2 * LOCAL, ROWS_A, ROWS_B)

    def wait_sib_a(k, slot):
        a_sib(slot, along_y(k), 1 - core).wait_recv()

    def wait_sib_b(k, slot):
        b_sib(slot, along_x(k), 1 - core).wait_recv()

    own_a.wait()
    for c in a1:
        c.wait_recv()
    go(a_right(0, 0, NX, y))
    go(a_left(0, 0, NX, y))
    go(a_sib(0, y, core))

    acc[...] = jnp.zeros_like(acc)
    sq[...] = jnp.zeros_like(sq)
    for p in params:
        p.wait()
    first_token = block * ROWS
    start, first_in, last_in, last_before = jnp.int32(0), jnp.int32(ROWS), jnp.int32(-1), jnp.int32(-1)
    starts = []
    for i in range(docs.shape[0]):
        here = start - first_token
        starts.append(here)
        inside = jnp.logical_and(here >= 0, here < ROWS)
        first_in = jnp.where(inside, jnp.minimum(first_in, here), first_in)
        last_in = jnp.where(inside, jnp.maximum(last_in, here), last_in)
        last_before = jnp.where(here < 0, jnp.maximum(last_before, start), last_before)
        start = start + docs[i]
    rate = pole[...]
    lam = jnp.exp(-rate)
    r2 = rate * rate
    series = 2.0 * jnp.exp(-rate) * rate * (
        1.0 + r2 * (1.0 / 6.0) * (1.0 + r2 * (1.0 / 20.0) * (1.0 + r2 * (1.0 / 42.0) * (1.0 + r2 * (1.0 / 72.0))))
    )
    mix = resid[...] * jnp.sqrt(jnp.where(rate < 0.5, series, 1.0 - jnp.exp(-2.0 * rate)))

    def end_weight(t, _):
        on = jnp.where(t >= last_in, 1.0, 0.0)
        sw[t] = jnp.exp(rate * (t - (ROWS - 1)).astype(F32)) * on
        return 0

    lax.fori_loop(0, ROWS, end_weight, 0, unroll=4)

    own_b.wait()
    for k in range(1, NY):
        b1[k].wait_recv()
    go(b_right(0, 0, NY, x))
    go(b_left(0, 0, NY, x))
    go(b_sib(0, x, core))

    a_right(0, 0, NX, along_y(-1)).wait_recv()
    go(a_right(1, 0, NX, along_y(-1)))
    go(a_sib(1, along_y(-1), core))
    a_left(0, 0, NX, along_y(1)).wait_recv()
    go(a_left(1, 0, NX, along_y(1)))
    go(a_sib(2, along_y(1), core))

    def from_before(t, _):
        on = jnp.where(t < first_in, 1.0, 0.0)
        t2[t] = mix * jnp.exp(rate * (-1 - t).astype(F32)) * on
        return 0

    lax.fori_loop(0, ROWS, from_before, 0, unroll=4)

    for p in parts:
        p.wait()
    wait_sib_a(0, 0)
    dots_a(0)

    a_right(1, 0, NX, along_y(-2)).wait_recv()
    go(a_right(2, 0, NX, along_y(-2)))
    go(a_sib(3, along_y(-2), core))
    a_left(1, 0, NX, along_y(2)).wait_recv()
    go(a_left(2, 0, NX, along_y(2)))
    go(a_sib(4, along_y(2), core))

    def decay(t, _):
        is_start = functools.reduce(jnp.logical_or, [t == s for s in starts])
        lk[t] = lam * jnp.where(is_start, 0.0, 1.0)
        return 0

    lax.fori_loop(0, ROWS, decay, 0, unroll=4)

    b_right(0, 0, NY, along_x(-1)).wait_recv()
    go(b_right(1, 0, NY // 2, along_x(-1)))
    go(b_sib(1, along_x(-1), core))
    b_left(0, 0, NY, along_x(1)).wait_recv()
    go(b_left(1, NY // 2, NY, along_x(1)))
    go(b_sib(2, along_x(1), core))

    wait_sib_a(-1, 1)
    dots_a(-1)
    wait_sib_a(1, 2)
    dots_a(1)
    wait_sib_b(0, 0)
    dots_b(0)

    a_right(2, 0, NX, along_y(-3)).wait_recv()
    go(a_right(3, 0, NX // 2, along_y(-3)))
    go(a_sib(5, along_y(-3), core))
    a_left(2, 0, NX, along_y(3)).wait_recv()
    go(a_left(3, NX // 2, NX, along_y(3)))
    go(a_sib(6, along_y(3), core))

    for d in range(1, REACH + 1):
        on = jnp.where(last_before < first_token - (d - 1) * ROWS, 1.0, 0.0)
        gains[d - 1] = jnp.exp(rate * (-(d - 1.0) * ROWS)) * on

    wait_sib_a(-2, 3)
    dots_a(-2)
    wait_sib_a(2, 4)
    dots_a(2)

    a_right(3, 0, NX // 2, along_y(4)).wait_recv()
    a_left(3, NX // 2, NX, along_y(4)).wait_recv()
    go(a_sib(7, along_y(4), core))
    wait_sib_b(-1, 1)
    dots_b(-1)
    b_right(1, 0, NY // 2, along_x(2)).wait_recv()
    b_left(1, NY // 2, NY, along_x(2)).wait_recv()
    go(b_sib(3, along_x(2), core))
    wait_sib_b(1, 2)
    dots_b(1)
    wait_sib_a(-3, 5)
    dots_a(-3)
    wait_sib_a(3, 6)
    dots_a(3)
    wait_sib_a(4, 7)
    dots_a(4)
    wait_sib_b(2, 3)
    dots_b(2)

    rowscale = lax.rsqrt(jnp.sum(sq[...], axis=1, keepdims=True) / width + 1e-06)
    drv[...] = (acc[:, LOCAL:2 * LOCAL] * rowscale) * (acc[:, 2 * LOCAL:] * rowscale)

    def end_state(i, carry):
        even, odd = carry
        rows = drv[pl.ds(pl.multiple_of(i * 8, 8), 8), :]
        for r in range(0, 8, 2):
            even = even + sw[i * 8 + r] * rows[r:r + 1, :]
            odd = odd + sw[i * 8 + r + 1] * rows[r + 1:r + 2, :]
        return even, odd

    nought = jnp.zeros((MODES, LOCAL), F32)
    even, odd = lax.fori_loop(0, ROWS // 8, end_state, (nought, nought), unroll=2)
    mine[...] = even + odd
    zs = [
        remote(mine, got.at[d - 1], z_send.at[d - 1], z_recv.at[d - 1], {"ctx": along_z(d)})
        for d in range(1, REACH + 1)
    ]
    for c in zs:
        c.start()

    def scan(i, state):
        rows = drv[pl.ds(pl.multiple_of(i * 8, 8), 8), :]
        for r in range(8):
            state = lk[i * 8 + r] * state + rows[r:r + 1, :]
            terms = mix * state
            y8[pl.ds(pl.multiple_of((i * 8 + r) * 8, 8), 8), :] = terms[:8] + terms[8:]
        return state

    lax.fori_loop(0, ROWS // 8, scan, nought)
    drv[...] = skip[...] * drv[...] + functools.reduce(
        jnp.add, [y8[pl.ds(s, ROWS, stride=8), :] for s in range(8)]
    )
    acc[:, :LOCAL] = acc[:, :LOCAL] * rowscale

    before = nought
    for d in range(1, REACH + 1):
        zs[d - 1].wait_recv()
        before = before + gains[d - 1] * got[d - 1]

    def carried(t, _):
        terms = t2[t] * before
        y8[pl.ds(pl.multiple_of(t * 8, 8), 8), :] = terms[:8] + terms[8:]
        return 0

    lax.fori_loop(0, ROWS, carried, 0, unroll=8)
    total = drv[...] + functools.reduce(
        jnp.add, [y8[pl.ds(s, ROWS, stride=8), :] for s in range(8)]
    )
    out[...] = (acc[:, :LOCAL] * total).astype(out.dtype)

    for c in (*a1, *b1.values(), *sent, *zs):
        c.wait_send()


def per_device(n_ctx, stream, in_weight, pole_rate, residue, skip_gain, doc_lengths):
    width = in_weight.shape[0]
    hbm = pl.BlockSpec(memory_space=pltpu.MemorySpace.HBM)
    dma = pltpu.SemaphoreType.DMA
    vmem = pltpu.VMEM
    bf16 = jnp.bfloat16
    return pl.pallas_call(
        functools.partial(kernel, n_ctx, width),
        out_shape=jax.ShapeDtypeStruct((ROWS, LOCAL), bf16),
        in_specs=[hbm] * 6,
        out_specs=pl.BlockSpec(memory_space=pltpu.VMEM),
        scratch_shapes=[
            vmem((NY, 2, NX, ROWS_A, LOCAL), bf16),
            vmem((NX, 2, NY, ROWS_B, LOCAL), bf16),
            vmem((width, 3 * LOCAL), bf16),
            vmem((ROWS, 3 * LOCAL), F32),
            vmem((ROWS, LOCAL), F32),
            vmem((ROWS, LOCAL), F32),
            vmem((ROWS * 8, LOCAL), F32),
            vmem((ROWS, MODES, LOCAL), F32),
            vmem((ROWS, MODES, LOCAL), F32),
            vmem((ROWS, MODES, LOCAL), F32),
            vmem((MODES, LOCAL), F32),
            vmem((MODES, LOCAL), F32),
            vmem((1, LOCAL), F32),
            vmem((MODES, LOCAL), F32),
            vmem((REACH, MODES, LOCAL), F32),
            vmem((REACH, MODES, LOCAL), F32),
            pltpu.SMEM((doc_lengths.shape[0],), jnp.int32),
            dma((3,)), dma((4,)), dma((2,)),
            dma((NX - 1,)), dma((NX - 1,)), dma((NY - 1,)), dma((NY - 1,)),
            dma((4,)), dma((4,)), dma((4,)), dma((4,)),
            dma((2,)), dma((2,)), dma((2,)), dma((2,)),
            dma((NY,)), dma((NY,)), dma((NX,)), dma((NX,)),
            dma((REACH,)), dma((REACH,)),
        ],
        compiler_params=pltpu.CompilerParams(
            collective_id=0, has_side_effects=True, vmem_limit_bytes=40 << 20
        ),
        name="hyena",
    )(
        stream, jnp.transpose(in_weight, (1, 0, 2)), pole_rate.T, residue.T,
        skip_gain.reshape(1, LOCAL), doc_lengths,
    )


def solution(mesh):
    placed = (P("ctx", "ch"), P(None, None, "ch"), P("ch", None), P("ch", None), P("ch"), P())
    return jax.shard_map(
        functools.partial(per_device, mesh.shape["ctx"]),
        mesh=mesh, in_specs=placed, out_specs=P("ctx", "ch"), check_vma=False,
    )
```

time: 311 us -> 58.3 us (0.19)
  the two profiles are of different devices: /device:TPU:192 before, /device:TPU:8 now
where the time goes in v1:
time: 58.3 us; the launch traced here: 58 us
  Pallas kernels  51.1 us (88%)
  local copies, waits for them, and re-layouts  6.86 us (12%)
    pallas_call x1, Pallas kernels, per_device(): pl.pallas_call(functools.partial(kernel, n_ctx, width), out_shape=jax.Sha...  51.1 us
    unnamed x13, local copies, waits for them, and re-layouts  6.86 us

profile of v1, /device:TPU:8, one launch (start us, length us, event | category | flops | bytes accessed | tf_op | source)
XLA Modules:
  0.0 58.0 jit_solution(15236062459388598793)
XLA Ops:
  0.0 0.0 copy-start
  0.0 2.8 %copy-done = bf16[8192,3,128]{2,0,1:T(8,128)(2,1)S(1)} copy-done((bf16[8192,3,128]{2,0,1:T(8,128)(2,1)S(1)}, bf16[8192,3,128]{2,0,1:T(8,128)(2,1)}, u32[]{:S(2)}) %copy-start) | copy-done | bytes 6291480
  2.8 0.0 copy-start.1
  2.8 0.8 %copy-done.1 = bf16[128,128]{1,0:T(8,128)(2,1)S(1)} copy-done((bf16[128,128]{1,0:T(8,128)(2,1)S(1)}, bf16[128,128]{1,0:T(8,128)(2,1)}, u32[]{:S(2)}) %copy-start.1) | copy-done | bytes 32792
  3.5 0.0 copy-start.2
  3.5 0.7 %copy-done.2 = f32[128,16]{0,1:T(8,128)S(1)} copy-done((f32[128,16]{0,1:T(8,128)S(1)}, f32[128,16]{0,1:T(8,128)}, u32[]{:S(2)}) %copy-start.2) | copy-done | bytes 8216
  4.2 0.0 copy-start.3
  4.2 0.7 %copy-done.3 = f32[128,16]{0,1:T(8,128)S(1)} copy-done((f32[128,16]{0,1:T(8,128)S(1)}, f32[128,16]{0,1:T(8,128)}, u32[]{:S(2)}) %copy-start.3) | copy-done | bytes 8216
  4.9 0.0 copy-start.4
  4.9 0.7 %copy-done.4 = f32[128]{0:T(128)S(1)} copy-done((f32[128]{0:T(128)S(1)}, f32[128]{0:T(128)}, u32[]{:S(2)}) %copy-start.4) | copy-done | bytes 536
  5.6 0.0 copy-start.5
  5.6 0.7 %copy-done.5 = s32[8]{0:T(128)S(1)} copy-done((s32[8]{0:T(128)S(1)}, s32[8]{0:T(128)}, u32[]{:S(2)}) %copy-start.5) | copy-done | bytes 56
  6.3 51.1 %hyena.1 = bf16[128,128]{1,0:T(8,128)(2,1)S(1)} custom-call(bf16[128,128]{1,0:T(8,128)(2,1)S(1)} %copy-done.1, bf16[3,8192,128]{2,1,0:T(8,128)(2,1)S(1)} %bitcast.4, f32[16,128]{1,0:T(8,128)S(1)} %bitcast.5, f32[16,128]{1,0:T(8,128)S(1)} %bitcast.6, f32[1,128]{1,0:T(1,128)S(1)} %bitcast.7, s32[8]{0:T(128)S(1)} %copy-done.5), custom_call_target="tpu_custom_call" | custom-call | tf_op jit(solution)/shard_map/hyena/pallas_call | solution.py:347
  57.4 0.6 %copy.8 = bf16[128,128]{1,0:T(8,128)(2,1)} copy(bf16[128,128]{1,0:T(8,128)(2,1)S(1)} %hyena.1) | data formatting | bytes 65536
Async XLA Ops:
  0.0 2.8 %copy-start = (bf16[8192,3,128]{2,0,1:T(8,128)(2,1)S(1)}, bf16[8192,3,128]{2,0,1:T(8,128)(2,1)}, u32[]{:S(2)}) copy-start(bf16[8192,3,128]{2,0,1:T(8,128)(2,1)} %param.7) | copy-start | bytes 18874372
  2.8 0.8 %copy-start.1 = (bf16[128,128]{1,0:T(8,128)(2,1)S(1)}, bf16[128,128]{1,0:T(8,128)(2,1)}, u32[]{:S(2)}) copy-start(bf16[128,128]{1,0:T(8,128)(2,1)} %stream.1) | copy-start | bytes 98308
  3.5 0.7 %copy-start.2 = (f32[128,16]{0,1:T(8,128)S(1)}, f32[128,16]{0,1:T(8,128)}, u32[]{:S(2)}) copy-start(f32[128,16]{0,1:T(8,128)} %param.8) | copy-start | bytes 24580
  4.2 0.7 %copy-start.3 = (f32[128,16]{0,1:T(8,128)S(1)}, f32[128,16]{0,1:T(8,128)}, u32[]{:S(2)}) copy-start(f32[128,16]{0,1:T(8,128)} %param.9) | copy-start | bytes 24580
  4.9 0.7 %copy-start.4 = (f32[128]{0:T(128)S(1)}, f32[128]{0:T(128)}, u32[]{:S(2)}) copy-start(f32[128]{0:T(128)} %param.10) | copy-start | bytes 1540
  5.6 0.7 %copy-start.5 = (s32[8]{0:T(128)S(1)}, s32[8]{0:T(128)}, u32[]{:S(2)}) copy-start(s32[8]{0:T(128)} %docs_h.1) | copy-start | bytes 100

commit v2 on v1

--- a/solution.py
+++ b/solution.py
@@ -27,7 +27,7 @@
     ar_send, ar_recv, al_send, al_recv,
     br_send, br_recv, bl_send, bl_recv,
     as_send, as_recv, bs_send, bs_recv,
-    z_send, z_recv,
+    z_send, z_recv, z_ready,
 ):
     block = lax.axis_index("ctx")
     ch = lax.axis_index("ch")
@@ -43,9 +43,6 @@
 
     def along_y(k):
         return lax.rem(y + (k + NY), NY)
-
-    def along_z(k):
-        return lax.rem(block + (k + n_ctx), n_ctx)
 
     def remote(src, dst, send, recv, device):
         return pltpu.make_async_remote_copy(
@@ -71,17 +68,26 @@
         p.start()
 
     sibling = at(x, y, 1 - core)
-    z_offsets = sorted({k % n_ctx for d in range(1, REACH + 1) for k in (d, -d)})
     friends = [sibling]
     friends += [at(along_x(k), y, core) for k in range(1, NX)]
     friends += [at(x, along_y(k), core) for k in range(1, NY)]
-    friends += [{"ctx": along_z(k)} for k in z_offsets]
     barrier = pltpu.get_barrier_semaphore()
     for friend in friends:
         pl.semaphore_signal(barrier, inc=1, device_id=friend, device_id_type=MESH)
+
+    def if_later(d, action):
+        pl.when(block + d < n_ctx)(action)
+
+    def if_earlier(d, action):
+        pl.when(block >= d)(action)
+
+    for d in range(1, REACH + 1):
+        if_later(d, lambda d=d: pl.semaphore_signal(
+            barrier, inc=1, device_id={"ctx": block + d}, device_id_type=MESH))
     for p in parts:
         p.start()
-    pl.semaphore_wait(barrier, len(friends))
+    got[...] = jnp.zeros_like(got)
+    pl.semaphore_wait(barrier, len(friends) + jnp.minimum(block, REACH))
 
     a1 = [
         remote(stream.at[pl.ds(0, ROWS_A)], ga.at[y, core, x],
@@ -97,6 +103,10 @@
         c.start()
     for k in (1, 7, 2, 6, 3, 5, 4):
         b1[k].start()
+
+    for d in range(1, REACH + 1):
+        if_earlier(d, lambda d=d: pl.semaphore_signal(
+            z_ready.at[d - 1], inc=1, device_id={"ctx": block - d}, device_id_type=MESH))
 
     sent = []
 
@@ -298,11 +308,14 @@
     even, odd = lax.fori_loop(0, ROWS // 8, end_state, (nought, nought), unroll=2)
     mine[...] = even + odd
     zs = [
-        remote(mine, got.at[d - 1], z_send.at[d - 1], z_recv.at[d - 1], {"ctx": along_z(d)})
+        remote(mine, got.at[d - 1], z_send.at[d - 1], z_recv.at[d - 1], {"ctx": block + d})
         for d in range(1, REACH + 1)
     ]
-    for c in zs:
-        c.start()
+    for d in range(1, REACH + 1):
+        def to_later(d=d):
+            pl.semaphore_wait(z_ready.at[d - 1], 1)
+            zs[d - 1].start()
+        if_later(d, to_later)
 
     def scan(i, state):
         rows = drv[pl.ds(pl.multiple_of(i * 8, 8), 8), :]
@@ -320,7 +333,7 @@
 
     before = nought
     for d in range(1, REACH + 1):
-        zs[d - 1].wait_recv()
+        if_earlier(d, zs[d - 1].wait_recv)
         before = before + gains[d - 1] * got[d - 1]
 
     def carried(t, _):
@@ -334,8 +347,10 @@
     )
     out[...] = (acc[:, :LOCAL] * total).astype(out.dtype)
 
-    for c in (*a1, *b1.values(), *sent, *zs):
+    for c in (*a1, *b1.values(), *sent):
         c.wait_send()
+    for d in range(1, REACH + 1):
+        if_later(d, zs[d - 1].wait_send)
 
 
 def per_device(n_ctx, stream, in_weight, pole_rate, residue, skip_gain, doc_lengths):
@@ -372,10 +387,10 @@
             dma((4,)), dma((4,)), dma((4,)), dma((4,)),
             dma((2,)), dma((2,)), dma((2,)), dma((2,)),
             dma((NY,)), dma((NY,)), dma((NX,)), dma((NX,)),
-            dma((REACH,)), dma((REACH,)),
+            dma((REACH,)), dma((REACH,)), pltpu.SemaphoreType.REGULAR((REACH,)),
         ],
         compiler_params=pltpu.CompilerParams(
-            collective_id=0, has_side_effects=True, vmem_limit_bytes=40 << 20
+            collective_id=0, has_side_effects=True, vmem_limit_bytes=60 << 20
         ),
         name="hyena",
     )(

time: 58.3 us -> 40.4 us (0.69)
  the two profiles are of different devices: /device:TPU:8 before, /device:TPU:64 now
where the time goes in v2:
time: 40.4 us; the launch traced here: 40.2 us
  Pallas kernels  38.8 us (96%)
  local copies, waits for them, and re-layouts  1.38 us (3%)
    pallas_call x1, Pallas kernels, per_device(): pl.pallas_call(functools.partial(kernel, n_ctx, width), out_shape=jax.Sha...  38.8 us
    unnamed x1, local copies, waits for them, and re-layouts  1.38 us

profile of v2, /device:TPU:64, one launch (start us, length us, event | category | flops | bytes accessed | tf_op | source)
XLA Modules:
  0.0 40.2 jit_solution(17768218208878719234)
XLA Ops:
  0.0 38.8 %hyena.1 = bf16[128,128]{1,0:T(8,128)(2,1)} custom-call(bf16[128,128]{1,0:T(8,128)(2,1)} %stream.1, bf16[3,8192,128]{2,1,0:T(8,128)(2,1)} %bitcast.4, f32[16,128]{1,0:T(8,128)} %bitcast.5, f32[16,128]{1,0:T(8,128)} %bitcast.6, f32[1,128]{1,0:T(1,128)} %bitcast.7, s32[8]{0:T(128)} %docs_h.1), custom_call_target="tpu_custom_call" | custom-call | tf_op jit(solution)/shard_map/hyena/pallas_call | solution.py:362
  38.8 1.4 %copy.8 = bf16[128,128]{1,0:T(8,128)(2,1)} copy(bf16[128,128]{1,0:T(8,128)(2,1)} %hyena.1) | data formatting | bytes 65536

commit v3 on v2

v3 whole, which is shorter than its diff:
```python
import functools

import jax
import jax.numpy as jnp
from jax import lax
from jax.experimental import pallas as pl
from jax.experimental.pallas import tpu as pltpu
from jax.sharding import PartitionSpec as P

MESH = pl.DeviceIdType.MESH
NX, NY = 4, 8
ROWS = 128
LOCAL = 128
MODES = 16
OFFSETS = (0, 1, -1, 2, -2, 3, -3, 4)
GROUPS = ((0, 1), (1, 3), (3, 5), (5, 7), (7, 8))
COLUMNS = (0, 1, -1, 2)
REACH = 6
F32 = jnp.float32


def kernel(
    n_ctx, width,
    stream, w3, pole_h, resid_h, skip_h, docs_h, out,
    g, w, acc, sq, drv, y8, sw, lk, t2, pole, resid, skip, mine, got, gains, docs,
    w_sem, prm_sem, own_sem,
    y_send, y_recv, xr_send, xr_recv, xl_send, xl_recv,
    x2r_send, x2r_recv, x2l_send, x2l_recv,
    s0_send, s0_recv, s1_send, s1_recv, s2_send, s2_recv,
    z_send, z_recv, z_ready,
):
    block = lax.axis_index("ctx")
    ch = lax.axis_index("ch")
    core = lax.rem(ch, 2)
    y = lax.rem(ch // 2, NY)
    x = ch // (2 * NY)

    def at(px, py, pc):
        return {"ch": (px * NY + py) * 2 + pc}

    def along_x(k):
        return lax.rem(x + (k + NX), NX)

    def along_y(k):
        return lax.rem(y + (k + NY), NY)

    def remote(src, dst, send, recv, device):
        return pltpu.make_async_remote_copy(
            src_ref=src, dst_ref=dst, send_sem=send, recv_sem=recv,
            device_id=device, device_id_type=MESH,
        )

    parts = [
        pltpu.make_async_copy(w3.at[j], w.at[:, pl.ds(j * LOCAL, LOCAL)], w_sem.at[j])
        for j in range(3)
    ]
    params = [
        pltpu.make_async_copy(src, dst, prm_sem.at[i])
        for i, (src, dst) in enumerate(
            ((pole_h, pole), (resid_h, resid), (skip_h, skip), (docs_h, docs))
        )
    ]
    own = pltpu.make_async_copy(stream, g.at[core, 0, 0], own_sem)
    own.start()
    for p in params:
        p.start()

    sibling = at(x, y, 1 - core)
    friends = [sibling]
    friends += [at(along_x(k), y, core) for k in (1, -1)]
    friends += [at(x, along_y(k), core) for k in range(1, NY)]
    barrier = pltpu.get_barrier_semaphore()
    for friend in friends:
        pl.semaphore_signal(barrier, inc=1, device_id=friend, device_id_type=MESH)

    def if_later(d, action):
        pl.when(block + d < n_ctx)(action)

    def if_earlier(d, action):
        pl.when(block >= d)(action)

    for d in range(1, REACH + 1):
        if_later(d, lambda d=d: pl.semaphore_signal(
            barrier, inc=1, device_id={"ctx": block + d}, device_id_type=MESH))
    for p in parts:
        p.start()
    got[...] = jnp.zeros_like(got)
    pl.semaphore_wait(barrier, len(friends) + jnp.minimum(block, REACH))

    sent = []

    def go(copy):
        copy.start()
        sent.append(copy)

    def same(ref, send, recv, device):
        return remote(ref, ref, send, recv, device)

    def y_copy(k):
        slot = OFFSETS.index(-k if k < 4 else 4)
        return remote(stream, g.at[core, 0, slot], y_send.at[slot - 1], y_recv.at[slot - 1],
                      at(x, along_y(k), core))

    def x_right(i):
        lo, hi = GROUPS[i]
        src = stream if i == 0 else g.at[core, 0, pl.ds(lo, hi - lo)]
        dst = g.at[core, 2, 0] if i == 0 else g.at[core, 2, pl.ds(lo, hi - lo)]
        return remote(src, dst, xr_send.at[i], xr_recv.at[i], at(along_x(1), y, core))

    def x_left(i):
        lo, hi = GROUPS[i]
        src = stream if i == 0 else g.at[core, 0, pl.ds(lo, hi - lo)]
        dst = g.at[core, 1, 0] if i == 0 else g.at[core, 1, pl.ds(lo, hi - lo)]
        return remote(src, dst, xl_send.at[i], xl_recv.at[i], at(along_x(-1), y, core))

    def half(column, i, side):
        lo, hi = GROUPS[i]
        if hi - lo == 2:
            return g.at[core, column, lo + side]
        return g.at[core, column, lo, pl.ds(side * (ROWS // 2), ROWS // 2)]

    def x2_right(i):
        return remote(half(2, i, 0), half(3, i, 0), x2r_send.at[i], x2r_recv.at[i], at(along_x(1), y, core))

    def x2_left(i):
        return remote(half(1, i, 1), half(3, i, 1), x2l_send.at[i], x2l_recv.at[i], at(along_x(-1), y, core))

    def sib(column, i, c):
        lo, hi = GROUPS[i]
        slots = pl.ds(lo, hi - lo)
        if column == 0:
            return same(g.at[c, 0, slots], s0_send.at[i], s0_recv.at[i], sibling)
        if column == 1:
            return same(g.at[c, pl.ds(1, 2), slots], s1_send.at[i], s1_recv.at[i], sibling)
        return same(g.at[c, 3, slots], s2_send.at[i], s2_recv.at[i], sibling)

    go(x_right(0))
    go(x_left(0))
    for k in (1, -1, 2, -2, 3, -3, 4):
        go(y_copy(k))
    for d in range(1, REACH + 1):
        if_earlier(d, lambda d=d: pl.semaphore_signal(
            z_ready.at[d - 1], inc=1, device_id={"ctx": block - d}, device_id_type=MESH))

    own.wait()
    go(sib(0, 0, core))

    def dots(column, i):
        columns = (1, 2) if column == 1 else (column,)
        for c in columns:
            for slot in range(*GROUPS[i]):
                chip = along_x(COLUMNS[c]) * NY + along_y(OFFSETS[slot])
                lhs = jnp.concatenate([g[0, c, slot], g[1, c, slot]], axis=1)
                rows = pl.ds(pl.multiple_of(chip * (2 * LOCAL), 2 * LOCAL), 2 * LOCAL)
                acc[...] += jnp.dot(lhs, w[rows, :], preferred_element_type=F32)
                f = lhs.astype(F32)
                f = f * f
                sq[...] += f[:, :LOCAL] + f[:, LOCAL:]

    def col0(i):
        for slot in range(*GROUPS[i]):
            k = OFFSETS[slot]
            y_copy(4 if k == 4 else -k).wait_recv()
        go(x_right(i))
        go(x_left(i))
        go(sib(0, i, core))

    def col1(i):
        x_right(i).wait_recv()
        go(x2_right(i))
        x_left(i).wait_recv()
        go(x2_left(i))
        go(sib(1, i, core))

    def col2(i):
        x2_right(i).wait_recv()
        x2_left(i).wait_recv()
        go(sib(3, i, core))

    def use(column, i):
        sib(column, i, 1 - core).wait_recv()
        dots(column, i)

    acc[...] = jnp.zeros_like(acc)
    sq[...] = jnp.zeros_like(sq)
    for p in params:
        p.wait()
    first_token = block * ROWS
    start, first_in, last_in, last_before = jnp.int32(0), jnp.int32(ROWS), jnp.int32(-1), jnp.int32(-1)
    starts = []
    for i in range(docs.shape[0]):
        here = start - first_token
        starts.append(here)
        inside = jnp.logical_and(here >= 0, here < ROWS)
        first_in = jnp.where(inside, jnp.minimum(first_in, here), first_in)
        last_in = jnp.where(inside, jnp.maximum(last_in, here), last_in)
        last_before = jnp.where(here < 0, jnp.maximum(last_before, start), last_before)
        start = start + docs[i]
    rate = pole[...]
    lam = jnp.exp(-rate)
    r2 = rate * rate
    series = 2.0 * jnp.exp(-rate) * rate * (
        1.0 + r2 * (1.0 / 6.0) * (1.0 + r2 * (1.0 / 20.0) * (1.0 + r2 * (1.0 / 42.0) * (1.0 + r2 * (1.0 / 72.0))))
    )
    mix = resid[...] * jnp.sqrt(jnp.where(rate < 0.5, series, 1.0 - jnp.exp(-2.0 * rate)))

    def end_weight(t, _):
        on = jnp.where(t >= last_in, 1.0, 0.0)
        sw[t] = jnp.exp(rate * (t - (ROWS - 1)).astype(F32)) * on
        return 0

    def from_before(t, _):
        on = jnp.where(t < first_in, 1.0, 0.0)
        t2[t] = mix * jnp.exp(rate * (-1 - t).astype(F32)) * on
        return 0

    def decay(t, _):
        is_start = functools.reduce(jnp.logical_or, [t == s for s in starts])
        lk[t] = lam * jnp.where(is_start, 0.0, 1.0)
        return 0

    lax.fori_loop(0, ROWS, end_weight, 0, unroll=8)
    col0(1)
    col1(0)
    col0(2)
    lax.fori_loop(0, ROWS, from_before, 0, unroll=8)
    for p in parts:
        p.wait()
    use(0, 0)
    col1(1)
    col0(3)
    col2(0)
    use(0, 1)
    col0(4)
    col1(2)
    col2(1)
    lax.fori_loop(0, ROWS, decay, 0, unroll=8)
    for d in range(1, REACH + 1):
        on = jnp.where(last_before < first_token - (d - 1) * ROWS, 1.0, 0.0)
        gains[d - 1] = jnp.exp(rate * (-(d - 1.0) * ROWS)) * on
    use(1, 0)
    use(0, 2)
    use(3, 0)
    col1(3)
    col2(2)
    use(1, 1)
    use(0, 3)
    col1(4)
    col2(3)
    use(0, 4)
    use(3, 1)
    use(1, 2)
    use(3, 2)
    col2(4)
    use(1, 3)
    use(1, 4)
    use(3, 3)
    use(3, 4)

    rowscale = lax.rsqrt(jnp.sum(sq[...], axis=1, keepdims=True) / width + 1e-06)
    drv[...] = (acc[:, LOCAL:2 * LOCAL] * rowscale) * (acc[:, 2 * LOCAL:] * rowscale)

    def end_state(i, carry):
        even, odd = carry
        rows = drv[pl.ds(pl.multiple_of(i * 8, 8), 8), :]
        for r in range(0, 8, 2):
            even = even + sw[i * 8 + r] * rows[r:r + 1, :]
            odd = odd + sw[i * 8 + r + 1] * rows[r + 1:r + 2, :]
        return even, odd

    nought = jnp.zeros((MODES, LOCAL), F32)
    even, odd = lax.fori_loop(0, ROWS // 8, end_state, (nought, nought), unroll=2)
    mine[...] = even + odd
    zs = [
        remote(mine, got.at[d - 1], z_send.at[d - 1], z_recv.at[d - 1], {"ctx": block + d})
        for d in range(1, REACH + 1)
    ]
    for d in range(1, REACH + 1):
        def to_later(d=d):
            pl.semaphore_wait(z_ready.at[d - 1], 1)
            zs[d - 1].start()
        if_later(d, to_later)

    def scan(i, state):
        rows = drv[pl.ds(pl.multiple_of(i * 8, 8), 8), :]
        for r in range(8):
            state = lk[i * 8 + r] * state + rows[r:r + 1, :]
            terms = mix * state
            y8[pl.ds(pl.multiple_of((i * 8 + r) * 8, 8), 8), :] = terms[:8] + terms[8:]
        return state

    lax.fori_loop(0, ROWS // 8, scan, nought)
    drv[...] = skip[...] * drv[...] + functools.reduce(
        jnp.add, [y8[pl.ds(s, ROWS, stride=8), :] for s in range(8)]
    )
    acc[:, :LOCAL] = acc[:, :LOCAL] * rowscale

    before = nought
    for d in range(1, REACH + 1):
        if_earlier(d, zs[d - 1].wait_recv)
        before = before + gains[d - 1] * got[d - 1]

    def carried(t, _):
        terms = t2[t] * before
        y8[pl.ds(pl.multiple_of(t * 8, 8), 8), :] = terms[:8] + terms[8:]
        return 0

    lax.fori_loop(0, ROWS, carried, 0, unroll=8)
    total = drv[...] + functools.reduce(
        jnp.add, [y8[pl.ds(s, ROWS, stride=8), :] for s in range(8)]
    )
    out[...] = (acc[:, :LOCAL] * total).astype(out.dtype)

    for c in sent:
        c.wait_send()
    for d in range(1, REACH + 1):
        if_later(d, zs[d - 1].wait_send)


def per_device(n_ctx, stream, in_weight, pole_rate, residue, skip_gain, doc_lengths):
    width = in_weight.shape[0]
    hbm = pl.BlockSpec(memory_space=pltpu.MemorySpace.HBM)
    dma = pltpu.SemaphoreType.DMA
    vmem = pltpu.VMEM
    bf16 = jnp.bfloat16
    return pl.pallas_call(
        functools.partial(kernel, n_ctx, width),
        out_shape=jax.ShapeDtypeStruct((ROWS, LOCAL), bf16),
        in_specs=[hbm] * 6,
        out_specs=pl.BlockSpec(memory_space=pltpu.VMEM),
        scratch_shapes=[
            vmem((2, NX, NY, ROWS, LOCAL), bf16),
            vmem((width, 3 * LOCAL), bf16),
            vmem((ROWS, 3 * LOCAL), F32),
            vmem((ROWS, LOCAL), F32),
            vmem((ROWS, LOCAL), F32),
            vmem((ROWS * 8, LOCAL), F32),
            vmem((ROWS, MODES, LOCAL), F32),
            vmem((ROWS, MODES, LOCAL), F32),
            vmem((ROWS, MODES, LOCAL), F32),
            vmem((MODES, LOCAL), F32),
            vmem((MODES, LOCAL), F32),
            vmem((1, LOCAL), F32),
            vmem((MODES, LOCAL), F32),
            vmem((REACH, MODES, LOCAL), F32),
            vmem((REACH, MODES, LOCAL), F32),
            pltpu.SMEM((doc_lengths.shape[0],), jnp.int32),
            dma((3,)), dma((4,)), dma,
            dma((NY - 1,)), dma((NY - 1,)),
            *[dma((len(GROUPS),))] * 14,
            dma((REACH,)), dma((REACH,)), pltpu.SemaphoreType.REGULAR((REACH,)),
        ],
        compiler_params=pltpu.CompilerParams(
            collective_id=0, has_side_effects=True, vmem_limit_bytes=60 << 20
        ),
        name="hyena",
    )(
        stream, jnp.transpose(in_weight, (1, 0, 2)), pole_rate.T, residue.T,
        skip_gain.reshape(1, LOCAL), doc_lengths,
    )


def solution(mesh):
    placed = (P("ctx", "ch"), P(None, None, "ch"), P("ch", None), P("ch", None), P("ch"), P())
    return jax.shard_map(
        functools.partial(per_device, mesh.shape["ctx"]),
        mesh=mesh, in_specs=placed, out_specs=P("ctx", "ch"), check_vma=False,
    )
```

time: 40.4 us -> 34.9 us (0.86)
  the two profiles are of different devices: /device:TPU:64 before, /device:TPU:1 now
where the time goes in v3:
time: 34.9 us; the launch traced here: 34.4 us
  Pallas kernels  33 us (95%)
  local copies, waits for them, and re-layouts  1.38 us (4%)
    pallas_call x1, Pallas kernels, per_device(): pl.pallas_call(functools.partial(kernel, n_ctx, width), out_shape=jax.Sha...  33 us
    unnamed x1, local copies, waits for them, and re-layouts  1.38 us

profile of v3, /device:TPU:1, one launch (start us, length us, event | category | flops | bytes accessed | tf_op | source)
XLA Modules:
  0.0 34.4 jit_solution(16413040968952897478)
XLA Ops:
  0.0 33.0 %hyena.1 = bf16[128,128]{1,0:T(8,128)(2,1)} custom-call(bf16[128,128]{1,0:T(8,128)(2,1)} %stream.1, bf16[3,8192,128]{2,1,0:T(8,128)(2,1)} %bitcast.4, f32[16,128]{1,0:T(8,128)} %bitcast.5, f32[16,128]{1,0:T(8,128)} %bitcast.6, f32[1,128]{1,0:T(1,128)} %bitcast.7, s32[8]{0:T(128)} %docs_h.1), custom_call_target="tpu_custom_call" | custom-call | tf_op jit(solution)/shard_map/hyena/pallas_call | solution.py:326
  33.0 1.4 %copy.8 = bf16[128,128]{1,0:T(8,128)(2,1)} copy(bf16[128,128]{1,0:T(8,128)(2,1)} %hyena.1) | data formatting | bytes 65536

commit v4 on v3

--- a/solution.py
+++ b/solution.py
@@ -14,6 +14,7 @@
 MODES = 16
 OFFSETS = (0, 1, -1, 2, -2, 3, -3, 4)
 GROUPS = ((0, 1), (1, 3), (3, 5), (5, 7), (7, 8))
+BY_Y = 1
 COLUMNS = (0, 1, -1, 2)
 REACH = 6
 F32 = jnp.float32
@@ -24,9 +25,7 @@
     stream, w3, pole_h, resid_h, skip_h, docs_h, out,
     g, w, acc, sq, drv, y8, sw, lk, t2, pole, resid, skip, mine, got, gains, docs,
     w_sem, prm_sem, own_sem,
-    y_send, y_recv, xr_send, xr_recv, xl_send, xl_recv,
-    x2r_send, x2r_recv, x2l_send, x2l_recv,
-    s0_send, s0_recv, s1_send, s1_recv, s2_send, s2_recv,
+    y_send, y_recv, x_send, x_recv, f_send, f_recv, s_send, s_recv,
     z_send, z_recv, z_ready,
 ):
     block = lax.axis_index("ctx")
@@ -67,8 +66,8 @@
 
     sibling = at(x, y, 1 - core)
     friends = [sibling]
-    friends += [at(along_x(k), y, core) for k in (1, -1)]
-    friends += [at(x, along_y(k), core) for k in range(1, NY)]
+    friends += [at(along_x(k), y, core) for k in (1, -1, 2)]
+    friends += [at(x, along_y(k), core) for k in (1, -1, 2, -2)]
     barrier = pltpu.get_barrier_semaphore()
     for friend in friends:
         pl.semaphore_signal(barrier, inc=1, device_id=friend, device_id_type=MESH)
@@ -82,6 +81,7 @@
     for d in range(1, REACH + 1):
         if_later(d, lambda d=d: pl.semaphore_signal(
             barrier, inc=1, device_id={"ctx": block + d}, device_id_type=MESH))
+    own.wait()
     for p in parts:
         p.start()
     got[...] = jnp.zeros_like(got)
@@ -96,58 +96,58 @@
     def same(ref, send, recv, device):
         return remote(ref, ref, send, recv, device)
 
+    low, high = pl.ds(0, ROWS // 2), pl.ds(ROWS // 2, ROWS // 2)
+
     def y_copy(k):
-        slot = OFFSETS.index(-k if k < 4 else 4)
-        return remote(stream, g.at[core, 0, slot], y_send.at[slot - 1], y_recv.at[slot - 1],
+        slot = OFFSETS.index(-k)
+        return remote(g.at[core, 0, 0], g.at[core, 0, slot], y_send.at[slot - 1], y_recv.at[slot - 1],
                       at(x, along_y(k), core))
 
-    def x_right(i):
-        lo, hi = GROUPS[i]
-        src = stream if i == 0 else g.at[core, 0, pl.ds(lo, hi - lo)]
-        dst = g.at[core, 2, 0] if i == 0 else g.at[core, 2, pl.ds(lo, hi - lo)]
-        return remote(src, dst, xr_send.at[i], xr_recv.at[i], at(along_x(1), y, core))
-
-    def x_left(i):
-        lo, hi = GROUPS[i]
-        src = stream if i == 0 else g.at[core, 0, pl.ds(lo, hi - lo)]
-        dst = g.at[core, 1, 0] if i == 0 else g.at[core, 1, pl.ds(lo, hi - lo)]
-        return remote(src, dst, xl_send.at[i], xl_recv.at[i], at(along_x(-1), y, core))
-
-    def half(column, i, side):
-        lo, hi = GROUPS[i]
-        if hi - lo == 2:
-            return g.at[core, column, lo + side]
-        return g.at[core, column, lo, pl.ds(side * (ROWS // 2), ROWS // 2)]
-
-    def x2_right(i):
-        return remote(half(2, i, 0), half(3, i, 0), x2r_send.at[i], x2r_recv.at[i], at(along_x(1), y, core))
-
-    def x2_left(i):
-        return remote(half(1, i, 1), half(3, i, 1), x2l_send.at[i], x2l_recv.at[i], at(along_x(-1), y, core))
-
-    def sib(column, i, c):
-        lo, hi = GROUPS[i]
-        slots = pl.ds(lo, hi - lo)
-        if column == 0:
-            return same(g.at[c, 0, slots], s0_send.at[i], s0_recv.at[i], sibling)
-        if column == 1:
-            return same(g.at[c, pl.ds(1, 2), slots], s1_send.at[i], s1_recv.at[i], sibling)
-        return same(g.at[c, 3, slots], s2_send.at[i], s2_recv.at[i], sibling)
-
-    go(x_right(0))
-    go(x_left(0))
-    for k in (1, -1, 2, -2, 3, -3, 4):
+    def y_third(k):
+        src, dst = OFFSETS.index(-2 * k), OFFSETS.index(-3 * k)
+        return remote(g.at[core, 0, src], g.at[core, 0, dst], y_send.at[dst - 1], y_recv.at[dst - 1],
+                      at(x, along_y(k), core))
+
+    def y_fourth(k):
+        rows, i = (low, 6) if k > 0 else (high, 7)
+        return remote(g.at[core, 0, OFFSETS.index(-2 * k), rows], g.at[core, 0, 7, rows],
+                      y_send.at[i], y_recv.at[i], at(x, along_y(2 * k), core))
+
+    def x_copy(i, k):
+        slots = pl.ds(GROUPS[i][0], GROUPS[i][1] - GROUPS[i][0])
+        column = COLUMNS.index(2 if k == 2 else -k)
+        n = 3 * i + column - 1
+        return remote(g.at[core, 0, slots], g.at[core, column, slots], x_send.at[n], x_recv.at[n],
+                      at(along_x(k), y, core))
+
+    def row_copy(k):
+        slot = OFFSETS.index(-k)
+        columns = pl.ds(1, NX - 1)
+        return remote(g.at[core, columns, 0], g.at[core, columns, slot], f_send.at[slot - 1], f_recv.at[slot - 1],
+                      at(x, along_y(k), core))
+
+    def sib(row, i, c):
+        slots = pl.ds(GROUPS[i][0], GROUPS[i][1] - GROUPS[i][0])
+        columns = pl.ds(1, NX - 1) if row else pl.ds(0, 1)
+        ref = g.at[c, columns, slots]
+        n = len(GROUPS) * row + i
+        return remote(ref, ref, s_send.at[n], s_recv.at[n], sibling)
+
+    def x_all(i):
+        for k in (2, 1, -1):
+            go(x_copy(i, k))
+
+    x_all(0)
+    for k in (2, -2, 1, -1):
         go(y_copy(k))
     for d in range(1, REACH + 1):
         if_earlier(d, lambda d=d: pl.semaphore_signal(
             z_ready.at[d - 1], inc=1, device_id={"ctx": block - d}, device_id_type=MESH))
 
-    own.wait()
     go(sib(0, 0, core))
 
-    def dots(column, i):
-        columns = (1, 2) if column == 1 else (column,)
-        for c in columns:
+    def dots(row, i):
+        for c in range(1, NX) if row else (0,):
             for slot in range(*GROUPS[i]):
                 chip = along_x(COLUMNS[c]) * NY + along_y(OFFSETS[slot])
                 lhs = jnp.concatenate([g[0, c, slot], g[1, c, slot]], axis=1)
@@ -158,28 +158,39 @@
                 sq[...] += f[:, :LOCAL] + f[:, LOCAL:]
 
     def col0(i):
-        for slot in range(*GROUPS[i]):
-            k = OFFSETS[slot]
-            y_copy(4 if k == 4 else -k).wait_recv()
-        go(x_right(i))
-        go(x_left(i))
+        if i == 1:
+            y_copy(1).wait_recv()
+            y_copy(-1).wait_recv()
+        elif i == 2:
+            for k in (1, -1):
+                y_copy(2 * k).wait_recv()
+                go(y_fourth(k))
+                go(y_third(k))
+        elif i == 3:
+            y_third(1).wait_recv()
+            y_third(-1).wait_recv()
+        else:
+            y_fourth(1).wait_recv()
+            y_fourth(-1).wait_recv()
+        if i != BY_Y:
+            x_all(i)
         go(sib(0, i, core))
 
-    def col1(i):
-        x_right(i).wait_recv()
-        go(x2_right(i))
-        x_left(i).wait_recv()
-        go(x2_left(i))
+    def row(i):
+        if i == BY_Y:
+            row_copy(1).wait_recv()
+            row_copy(-1).wait_recv()
+        else:
+            for k in (1, -1, 2):
+                x_copy(i, k).wait_recv()
+        if i == 0:
+            go(row_copy(1))
+            go(row_copy(-1))
         go(sib(1, i, core))
 
-    def col2(i):
-        x2_right(i).wait_recv()
-        x2_left(i).wait_recv()
-        go(sib(3, i, core))
-
-    def use(column, i):
-        sib(column, i, 1 - core).wait_recv()
-        dots(column, i)
+    def use(row, i):
+        sib(row, i, 1 - core).wait_recv()
+        dots(row, i)
 
     acc[...] = jnp.zeros_like(acc)
     sq[...] = jnp.zeros_like(sq)
@@ -221,41 +232,31 @@
 
     lax.fori_loop(0, ROWS, end_weight, 0, unroll=8)
     col0(1)
-    col1(0)
     col0(2)
+    row(0)
     lax.fori_loop(0, ROWS, from_before, 0, unroll=8)
     for p in parts:
         p.wait()
     use(0, 0)
-    col1(1)
+    use(0, 1)
     col0(3)
-    col2(0)
-    use(0, 1)
     col0(4)
-    col1(2)
-    col2(1)
+    use(1, 0)
+    use(0, 2)
+    row(2)
+    row(1)
+    use(0, 3)
     lax.fori_loop(0, ROWS, decay, 0, unroll=8)
     for d in range(1, REACH + 1):
         on = jnp.where(last_before < first_token - (d - 1) * ROWS, 1.0, 0.0)
         gains[d - 1] = jnp.exp(rate * (-(d - 1.0) * ROWS)) * on
-    use(1, 0)
-    use(0, 2)
-    use(3, 0)
-    col1(3)
-    col2(2)
+    use(0, 4)
+    use(1, 2)
     use(1, 1)
-    use(0, 3)
-    col1(4)
-    col2(3)
-    use(0, 4)
-    use(3, 1)
-    use(1, 2)
-    use(3, 2)
-    col2(4)
+    row(3)
+    row(4)
     use(1, 3)
     use(1, 4)
-    use(3, 3)
-    use(3, 4)
 
     rowscale = lax.rsqrt(jnp.sum(sq[...], axis=1, keepdims=True) / width + 1e-06)
     drv[...] = (acc[:, LOCAL:2 * LOCAL] * rowscale) * (acc[:, 2 * LOCAL:] * rowscale)
@@ -275,7 +276,7 @@
         remote(mine, got.at[d - 1], z_send.at[d - 1], z_recv.at[d - 1], {"ctx": block + d})
         for d in range(1, REACH + 1)
     ]
-    for d in range(1, REACH + 1):
+    for d in range(REACH, 0, -1):
         def to_later(d=d):
             pl.semaphore_wait(z_ready.at[d - 1], 1)
             zs[d - 1].start()
@@ -346,8 +347,9 @@
             vmem((REACH, MODES, LOCAL), F32),
             pltpu.SMEM((doc_lengths.shape[0],), jnp.int32),
             dma((3,)), dma((4,)), dma,
-            dma((NY - 1,)), dma((NY - 1,)),
-            *[dma((len(GROUPS),))] * 14,
+            dma((NY,)), dma((NY,)),
+            dma((3 * len(GROUPS),)), dma((3 * len(GROUPS),)), dma((2,)), dma((2,)),
+            dma((2 * len(GROUPS),)), dma((2 * len(GROUPS),)),
             dma((REACH,)), dma((REACH,)), pltpu.SemaphoreType.REGULAR((REACH,)),
         ],
         compiler_params=pltpu.CompilerParams(

time: 34.9 us -> 31.3 us (0.90)
  Pallas kernels: 33 us -> 29.7 us
    pallas_call x1, Pallas kernels: 33 us -> 29.7 us  [per_device(): pl.pallas_call(functools.partial(kernel, n_ctx, width), out_shape=jax.Sha...]
where the time goes in v4:
time: 31.3 us; the launch traced here: 31 us
  Pallas kernels  29.7 us (95%)
  local copies, waits for them, and re-layouts  1.38 us (4%)
    pallas_call x1, Pallas kernels, per_device(): pl.pallas_call(functools.partial(kernel, n_ctx, width), out_shape=jax.Sha...  29.7 us
    unnamed x1, local copies, waits for them, and re-layouts  1.38 us

profile of v4, /device:TPU:1, one launch (start us, length us, event | category | flops | bytes accessed | tf_op | source)
XLA Modules:
  0.0 31.0 jit_solution(4861646181315228332)
XLA Ops:
  0.0 29.7 %hyena.1 = bf16[128,128]{1,0:T(8,128)(2,1)} custom-call(bf16[128,128]{1,0:T(8,128)(2,1)} %stream.1, bf16[3,8192,128]{2,1,0:T(8,128)(2,1)} %bitcast.4, f32[16,128]{1,0:T(8,128)} %bitcast.5, f32[16,128]{1,0:T(8,128)} %bitcast.6, f32[1,128]{1,0:T(1,128)} %bitcast.7, s32[8]{0:T(128)} %docs_h.1), custom_call_target="tpu_custom_call" | custom-call | tf_op jit(solution)/shard_map/hyena/pallas_call | solution.py:327
  29.7 1.4 %copy.8 = bf16[128,128]{1,0:T(8,128)(2,1)} copy(bf16[128,128]{1,0:T(8,128)(2,1)} %hyena.1) | data formatting | bytes 65536

commit v5 on v4

--- a/solution.py
+++ b/solution.py
@@ -23,7 +23,7 @@
 def kernel(
     n_ctx, width,
     stream, w3, pole_h, resid_h, skip_h, docs_h, out,
-    g, w, acc, sq, drv, y8, sw, lk, t2, pole, resid, skip, mine, got, gains, docs,
+    g, w, acc, sq, drv, y8, sw, lk, t2, mixes, pole, resid, skip, mine, got, gains, docs,
     w_sem, prm_sem, own_sem,
     y_send, y_recv, x_send, x_recv, f_send, f_recv, s_send, s_recv,
     z_send, z_recv, z_ready,
@@ -67,7 +67,7 @@
     sibling = at(x, y, 1 - core)
     friends = [sibling]
     friends += [at(along_x(k), y, core) for k in (1, -1, 2)]
-    friends += [at(x, along_y(k), core) for k in (1, -1, 2, -2)]
+    friends += [at(x, along_y(k), core) for k in range(1, NY)]
     barrier = pltpu.get_barrier_semaphore()
     for friend in friends:
         pl.semaphore_signal(barrier, inc=1, device_id=friend, device_id_type=MESH)
@@ -99,19 +99,9 @@
     low, high = pl.ds(0, ROWS // 2), pl.ds(ROWS // 2, ROWS // 2)
 
     def y_copy(k):
-        slot = OFFSETS.index(-k)
+        slot = OFFSETS.index(4 if k == 4 else -k)
         return remote(g.at[core, 0, 0], g.at[core, 0, slot], y_send.at[slot - 1], y_recv.at[slot - 1],
                       at(x, along_y(k), core))
-
-    def y_third(k):
-        src, dst = OFFSETS.index(-2 * k), OFFSETS.index(-3 * k)
-        return remote(g.at[core, 0, src], g.at[core, 0, dst], y_send.at[dst - 1], y_recv.at[dst - 1],
-                      at(x, along_y(k), core))
-
-    def y_fourth(k):
-        rows, i = (low, 6) if k > 0 else (high, 7)
-        return remote(g.at[core, 0, OFFSETS.index(-2 * k), rows], g.at[core, 0, 7, rows],
-                      y_send.at[i], y_recv.at[i], at(x, along_y(2 * k), core))
 
     def x_copy(i, k):
         slots = pl.ds(GROUPS[i][0], GROUPS[i][1] - GROUPS[i][0])
@@ -138,7 +128,7 @@
             go(x_copy(i, k))
 
     x_all(0)
-    for k in (2, -2, 1, -1):
+    for k in (1, -1, 2, -2, 3, -3, 4):
         go(y_copy(k))
     for d in range(1, REACH + 1):
         if_earlier(d, lambda d=d: pl.semaphore_signal(
@@ -158,20 +148,9 @@
                 sq[...] += f[:, :LOCAL] + f[:, LOCAL:]
 
     def col0(i):
-        if i == 1:
-            y_copy(1).wait_recv()
-            y_copy(-1).wait_recv()
-        elif i == 2:
-            for k in (1, -1):
-                y_copy(2 * k).wait_recv()
-                go(y_fourth(k))
-                go(y_third(k))
-        elif i == 3:
-            y_third(1).wait_recv()
-            y_third(-1).wait_recv()
-        else:
-            y_fourth(1).wait_recv()
-            y_fourth(-1).wait_recv()
+        for slot in range(*GROUPS[i]):
+            k = OFFSETS[slot]
+            y_copy(4 if k == 4 else -k).wait_recv()
         if i != BY_Y:
             x_all(i)
         go(sib(0, i, core))
@@ -220,9 +199,13 @@
         sw[t] = jnp.exp(rate * (t - (ROWS - 1)).astype(F32)) * on
         return 0
 
-    def from_before(t, _):
-        on = jnp.where(t < first_in, 1.0, 0.0)
-        t2[t] = mix * jnp.exp(rate * (-1 - t).astype(F32)) * on
+    mixes[...] = mix
+    token = lax.broadcasted_iota(jnp.int32, (ROWS, LOCAL), 0)
+    ages = (-1 - token).astype(F32)
+    on_before = jnp.where(token < first_in, 1.0, 0.0)
+
+    def from_before(n, _):
+        t2[n] = mixes[pl.ds(n, 1), :] * jnp.exp(pole[pl.ds(n, 1), :] * ages) * on_before
         return 0
 
     def decay(t, _):
@@ -234,7 +217,7 @@
     col0(1)
     col0(2)
     row(0)
-    lax.fori_loop(0, ROWS, from_before, 0, unroll=8)
+    lax.fori_loop(0, MODES, from_before, 0)
     for p in parts:
         p.wait()
     use(0, 0)
@@ -301,15 +284,9 @@
         if_earlier(d, zs[d - 1].wait_recv)
         before = before + gains[d - 1] * got[d - 1]
 
-    def carried(t, _):
-        terms = t2[t] * before
-        y8[pl.ds(pl.multiple_of(t * 8, 8), 8), :] = terms[:8] + terms[8:]
-        return 0
-
-    lax.fori_loop(0, ROWS, carried, 0, unroll=8)
-    total = drv[...] + functools.reduce(
-        jnp.add, [y8[pl.ds(s, ROWS, stride=8), :] for s in range(8)]
-    )
+    total = drv[...]
+    for n in range(MODES):
+        total = total + t2[n] * before[n:n + 1, :]
     out[...] = (acc[:, :LOCAL] * total).astype(out.dtype)
 
     for c in sent:
@@ -338,7 +315,8 @@
             vmem((ROWS * 8, LOCAL), F32),
             vmem((ROWS, MODES, LOCAL), F32),
             vmem((ROWS, MODES, LOCAL), F32),
-            vmem((ROWS, MODES, LOCAL), F32),
+            vmem((MODES, ROWS, LOCAL), F32),
+            vmem((MODES, LOCAL), F32),
             vmem((MODES, LOCAL), F32),
             vmem((MODES, LOCAL), F32),
             vmem((1, LOCAL), F32),

time: 31.3 us -> 30 us (0.958)
  Pallas kernels: 29.7 us -> 28.3 us
    pallas_call x1, Pallas kernels: 29.7 us -> 28.3 us  [per_device(): pl.pallas_call(functools.partial(kernel, n_ctx, width), out_shape=jax.Sha...]
where the time goes in v5:
time: 30 us; the launch traced here: 29.7 us
  Pallas kernels  28.3 us (94%)
  local copies, waits for them, and re-layouts  1.38 us (5%)
    pallas_call x1, Pallas kernels, per_device(): pl.pallas_call(functools.partial(kernel, n_ctx, width), out_shape=jax.Sha...  28.3 us
    unnamed x1, local copies, waits for them, and re-layouts  1.38 us

profile of v5, /device:TPU:1, one launch (start us, length us, event | category | flops | bytes accessed | tf_op | source)
XLA Modules:
  0.0 29.7 jit_solution(15900350312573051520)
XLA Ops:
  0.0 28.3 %hyena.1 = bf16[128,128]{1,0:T(8,128)(2,1)} custom-call(bf16[128,128]{1,0:T(8,128)(2,1)} %stream.1, bf16[3,8192,128]{2,1,0:T(8,128)(2,1)} %bitcast.4, f32[16,128]{1,0:T(8,128)} %bitcast.5, f32[16,128]{1,0:T(8,128)} %bitcast.6, f32[1,128]{1,0:T(1,128)} %bitcast.7, s32[8]{0:T(128)} %docs_h.1), custom_call_target="tpu_custom_call" | custom-call | tf_op jit(solution)/shard_map/hyena/pallas_call | solution.py:304
  28.3 1.4 %copy.8 = bf16[128,128]{1,0:T(8,128)(2,1)} copy(bf16[128,128]{1,0:T(8,128)(2,1)} %hyena.1) | data formatting | bytes 65536

commit v6 on v5

--- a/solution.py
+++ b/solution.py
@@ -23,7 +23,7 @@
 def kernel(
     n_ctx, width,
     stream, w3, pole_h, resid_h, skip_h, docs_h, out,
-    g, w, acc, sq, drv, y8, sw, lk, t2, mixes, pole, resid, skip, mine, got, gains, docs,
+    g, w, acc, sq, drv, y8, sw, lk, t2, t3, mixes, pole, resid, skip, mine, got, gains, docs,
     w_sem, prm_sem, own_sem,
     y_send, y_recv, x_send, x_recv, f_send, f_recv, s_send, s_recv,
     z_send, z_recv, z_ready,
@@ -127,9 +127,9 @@
         for k in (2, 1, -1):
             go(x_copy(i, k))
 
-    x_all(0)
     for k in (1, -1, 2, -2, 3, -3, 4):
         go(y_copy(k))
+    x_all(0)
     for d in range(1, REACH + 1):
         if_earlier(d, lambda d=d: pl.semaphore_signal(
             z_ready.at[d - 1], inc=1, device_id={"ctx": block - d}, device_id_type=MESH))
@@ -137,15 +137,20 @@
     go(sib(0, 0, core))
 
     def dots(row, i):
+        total = squares = None
         for c in range(1, NX) if row else (0,):
             for slot in range(*GROUPS[i]):
                 chip = along_x(COLUMNS[c]) * NY + along_y(OFFSETS[slot])
                 lhs = jnp.concatenate([g[0, c, slot], g[1, c, slot]], axis=1)
                 rows = pl.ds(pl.multiple_of(chip * (2 * LOCAL), 2 * LOCAL), 2 * LOCAL)
-                acc[...] += jnp.dot(lhs, w[rows, :], preferred_element_type=F32)
+                product = jnp.dot(lhs, w[rows, :], preferred_element_type=F32)
+                total = product if total is None else total + product
                 f = lhs.astype(F32)
                 f = f * f
-                sq[...] += f[:, :LOCAL] + f[:, LOCAL:]
+                f = f[:, :LOCAL] + f[:, LOCAL:]
+                squares = f if squares is None else squares + f
+        acc[...] += total
+        sq[...] += squares
 
     def col0(i):
         for slot in range(*GROUPS[i]):
@@ -177,11 +182,13 @@
         p.wait()
     first_token = block * ROWS
     start, first_in, last_in, last_before = jnp.int32(0), jnp.int32(ROWS), jnp.int32(-1), jnp.int32(-1)
-    starts = []
+    starts, first_second = [], jnp.int32(ROWS)
     for i in range(docs.shape[0]):
         here = start - first_token
         starts.append(here)
         inside = jnp.logical_and(here >= 0, here < ROWS)
+        late = jnp.logical_and(here >= ROWS // 2, here < ROWS)
+        first_second = jnp.where(late, jnp.minimum(first_second, here), first_second)
         first_in = jnp.where(inside, jnp.minimum(first_in, here), first_in)
         last_in = jnp.where(inside, jnp.maximum(last_in, here), last_in)
         last_before = jnp.where(here < 0, jnp.maximum(last_before, start), last_before)
@@ -206,6 +213,14 @@
 
     def from_before(n, _):
         t2[n] = mixes[pl.ds(n, 1), :] * jnp.exp(pole[pl.ds(n, 1), :] * ages) * on_before
+        return 0
+
+    second = lax.broadcasted_iota(jnp.int32, (ROWS // 2, LOCAL), 0)
+    second_ages = (-1 - second).astype(F32)
+    on_second = jnp.where(second + ROWS // 2 < first_second, 1.0, 0.0)
+
+    def from_first(n, _):
+        t3[n] = mixes[pl.ds(n, 1), :] * jnp.exp(pole[pl.ds(n, 1), :] * second_ages) * on_second
         return 0
 
     def decay(t, _):
@@ -230,6 +245,7 @@
     row(1)
     use(0, 3)
     lax.fori_loop(0, ROWS, decay, 0, unroll=8)
+    lax.fori_loop(0, MODES, from_first, 0)
     for d in range(1, REACH + 1):
         on = jnp.where(last_before < first_token - (d - 1) * ROWS, 1.0, 0.0)
         gains[d - 1] = jnp.exp(rate * (-(d - 1.0) * ROWS)) * on
@@ -265,18 +281,27 @@
             zs[d - 1].start()
         if_later(d, to_later)
 
-    def scan(i, state):
-        rows = drv[pl.ds(pl.multiple_of(i * 8, 8), 8), :]
+    half = ROWS // 2
+
+    def scan(i, states):
+        states = list(states)
+        rows = [drv[pl.ds(pl.multiple_of(h * half + i * 8, 8), 8), :] for h in range(2)]
         for r in range(8):
-            state = lk[i * 8 + r] * state + rows[r:r + 1, :]
-            terms = mix * state
-            y8[pl.ds(pl.multiple_of((i * 8 + r) * 8, 8), 8), :] = terms[:8] + terms[8:]
-        return state
-
-    lax.fori_loop(0, ROWS // 8, scan, nought)
+            for h in range(2):
+                t = h * half + i * 8 + r
+                states[h] = lk[t] * states[h] + rows[h][r:r + 1, :]
+                terms = mix * states[h]
+                y8[pl.ds(pl.multiple_of(t * 8, 8), 8), :] = terms[:8] + terms[8:]
+        return tuple(states)
+
+    middle, _ = lax.fori_loop(0, half // 8, scan, (nought, nought))
     drv[...] = skip[...] * drv[...] + functools.reduce(
         jnp.add, [y8[pl.ds(s, ROWS, stride=8), :] for s in range(8)]
     )
+    carried = drv[half:, :]
+    for n in range(MODES):
+        carried = carried + t3[n] * middle[n:n + 1, :]
+    drv[half:, :] = carried
     acc[:, :LOCAL] = acc[:, :LOCAL] * rowscale
 
     before = nought
@@ -316,6 +341,7 @@
             vmem((ROWS, MODES, LOCAL), F32),
             vmem((ROWS, MODES, LOCAL), F32),
             vmem((MODES, ROWS, LOCAL), F32),
+            vmem((MODES, ROWS // 2, LOCAL), F32),
             vmem((MODES, LOCAL), F32),
             vmem((MODES, LOCAL), F32),
             vmem((MODES, LOCAL), F32),

time: 30 us -> 30.4 us (1.013)
  Pallas kernels: 28.3 us -> 28.7 us
    pallas_call x1, Pallas kernels: 28.3 us -> 28.7 us  [per_device(): pl.pallas_call(functools.partial(kernel, n_ctx, width), out_shape=jax.Sha...]
where the time goes in v6:
time: 30.4 us; the launch traced here: 30.1 us
  Pallas kernels  28.7 us (94%)
  local copies, waits for them, and re-layouts  1.38 us (5%)
    pallas_call x1, Pallas kernels, per_device(): pl.pallas_call(functools.partial(kernel, n_ctx, width), out_shape=jax.Sha...  28.7 us
    unnamed x1, local copies, waits for them, and re-layouts  1.38 us

profile of v6, /device:TPU:1, one launch (start us, length us, event | category | flops | bytes accessed | tf_op | source)
XLA Modules:
  0.0 30.1 jit_solution(11087223494221639978)
XLA Ops:
  0.0 28.7 %hyena.1 = bf16[128,128]{1,0:T(8,128)(2,1)} custom-call(bf16[128,128]{1,0:T(8,128)(2,1)} %stream.1, bf16[3,8192,128]{2,1,0:T(8,128)(2,1)} %bitcast.4, f32[16,128]{1,0:T(8,128)} %bitcast.5, f32[16,128]{1,0:T(8,128)} %bitcast.6, f32[1,128]{1,0:T(1,128)} %bitcast.7, s32[8]{0:T(128)} %docs_h.1), custom_call_target="tpu_custom_call" | custom-call | tf_op jit(solution)/shard_map/hyena/pallas_call | solution.py:329
  28.7 1.4 %copy.8 = bf16[128,128]{1,0:T(8,128)(2,1)} copy(bf16[128,128]{1,0:T(8,128)(2,1)} %hyena.1) | data formatting | bytes 65536
